TPU v7x, 256 devices: a whole 4x4x8 slice. The times are simulated.
256 devices in a mesh: rows: 64 (over z, y, core), grp: 4 (over x).
Axes of the slice: x: 4, y: 4, z: 8, core: 2. Of those that a mesh axis runs over, the one named last changes fastest.
Arguments:
- a_diag: bfloat16 [512, 12, 128, 128], P('rows', 'grp'), may hold values from -1.25 to 1.25
- diag_cols: int32 [512, 12], P('rows', 'grp'), may hold values from 0 to 7
- a_offd: bfloat16 [512, 12, 128, 128], P('rows', 'grp'), may hold values from -1.25 to 1.25
- offd_cols: int32 [512, 12], P('rows', 'grp'), may hold values from 0 to 255, as said below
- prolong: bfloat16 [512, 2, 128, 128], P('rows'), may hold values from -0.5 to 0.5
- aggregate: int32 [512, 2], P('rows'), may hold values from 0 to 1, as said below
- send_rows: int32 [64, 64, 4], P('rows'), may hold values from 0 to 8, as said below
- ghost_agg: int32 [64, 64, 4, 2], P('rows'), may hold values from 0 to 1, as said below
- coarse_map: int32 [64, 98], P('rows'), may hold values from 0 to 127, as said below
Outputs:
- coarse: bfloat16 [128, 98, 128, 128], P('rows', None, 'grp')
Inputs may be any that keep to these rules, and one draw needn't show every extreme that they name: `send_rows`: for owner s and receiving node n, the block rows of s (0 to 7 within s) in the 4 slots of n; 8 marks an empty slot. A node receives from exactly 48 other nodes and never from itself; from each of them 4 - 1 to 4 distinct rows in the first slots, and 4 rows from at least one of them. `ghost_agg`: the aggregate entry of the sender's block row for each received tile; 0 in empty slots. `coarse_map`: distinct for each node, and holding every coarse id that a right factor of that node's products has. `aggregate`: distinct within a block row. `offd_cols`: always a filled slot of the node's received rows.
All inputs are finite; a program needn't handle non-finite values.
Results may differ from a plain program's by a relative error of at most 0.0049.
Values may be sent and summed in bfloat16 or wider, within the bound.
A program may use at most 128 MiB of HBM per device.

v0:
```python
import jax
import jax.numpy as jnp
from jax import lax
from jax.sharding import PartitionSpec as P

CR1 = 2


def slot_of(global_ids, col_map):
    positions = jnp.arange(col_map.shape[0], dtype=jnp.int32)
    return jnp.sum(jnp.where(global_ids[..., None] == col_map, positions, 0), axis=-1)


def galerkin_terms(running, a_tiles, right_tiles, slot_ids, left_tiles, targets):
    products_ab = jnp.einsum(
        "rkab,rkjbc->rkjac", a_tiles, right_tiles, preferred_element_type=jnp.float32
    ).astype(jnp.bfloat16)
    galerkin_part = jnp.einsum(
        "riaq,rkjac->rkijqc", left_tiles, products_ab, preferred_element_type=jnp.float32
    )
    index_shape = galerkin_part.shape[:4]
    rows_idx = jnp.broadcast_to(targets[:, None, :, None], index_shape)
    cols_idx = jnp.broadcast_to(slot_ids[:, :, None, :], index_shape)
    return running.at[rows_idx, cols_idx].add(galerkin_part)


def sweep(running, a_tiles, right_tiles, slot_ids, left_tiles, targets):
    row_count = a_tiles.shape[0]
    block_rows = 8
    turn_count = row_count // block_rows
    stacked = tuple(
        (
            item.reshape((turn_count, block_rows) + item.shape[1:])
            for item in (a_tiles, right_tiles, slot_ids, left_tiles, targets)
        )
    )

    def advance(carry, pieces):
        return (galerkin_terms(carry, *pieces), None)

    running, _ = lax.scan(advance, running, stacked)
    return running


def per_device(
    a_diag, diag_cols, a_offd, offd_cols, prolong, aggregate, send_rows, ghost_agg, coarse_map
):
    row_count, pieces, tile_size, _ = prolong.shape
    col_map = coarse_map[0]
    slot_total = col_map.shape[0]
    node_count, cap_slots = (send_rows.shape[1], send_rows.shape[2])
    node_index = lax.axis_index("rows")
    own_slots = slot_of(node_index * CR1 + aggregate, col_map)
    running = jnp.zeros((CR1, slot_total, tile_size, tile_size), jnp.float32)
    running = sweep(running, a_diag, prolong[diag_cols], own_slots[diag_cols], prolong, aggregate)
    padded = jnp.concatenate(
        [prolong, jnp.zeros((1, pieces, tile_size, tile_size), prolong.dtype)], axis=0
    )
    share_width = cap_slots // lax.axis_size("grp")
    my_slots = lax.dynamic_slice_in_dim(
        send_rows[0], lax.axis_index("grp") * share_width, share_width, 1
    )
    outgoing = jnp.take(padded, my_slots, axis=0)
    arrived = lax.all_to_all(outgoing, "rows", split_axis=0, concat_axis=0, tiled=True)
    arrived = lax.all_gather(arrived, "grp", axis=1, tiled=True)
    ghosts = arrived.reshape(node_count * cap_slots, pieces, tile_size, tile_size)
    sender_ids = jnp.arange(node_count, dtype=jnp.int32)
    ghost_ids = sender_ids[:, None, None] * CR1 + ghost_agg[0]
    ghost_slots = slot_of(ghost_ids, col_map).reshape(node_count * cap_slots, pieces)
    running = sweep(running, a_offd, ghosts[offd_cols], ghost_slots[offd_cols], prolong, aggregate)
    summed = lax.psum_scatter(running, "grp", scatter_dimension=2, tiled=True)
    return summed.astype(jnp.bfloat16)


def solution(mesh):
    in_specs = (
        P("rows", "grp", None, None),
        P("rows", "grp"),
        P("rows", "grp", None, None),
        P("rows", "grp"),
        P("rows", None, None, None),
        P("rows", None),
        P("rows", None, None),
        P("rows", None, None, None),
        P("rows", None),
    )
    out_specs = P("rows", None, "grp", None)
    return jax.shard_map(
        per_device, mesh=mesh, in_specs=in_specs, out_specs=out_specs, check_vma=False
    )
```

profile of v0, /device:TPU:1, one launch (start us, length us, event | category | flops | bytes accessed | tf_op | source)
XLA Modules:
  0.0 446.6 jit_solution(12985121202974713259)
XLA Ops:
  6.5 0.8 fusion.10
  7.3 0.7 compare_and_fusion
  8.0 1.1 concatenate.13
  9.1 3.0 gather_fusion.3
  12.1 2.6 bitcast_select_fusion
  14.8 107.7 %all_to_all.5 = bf16[64,1,2,128,128]{4,3,2,1,0:T(8,128)(2,1)} all-to-all(bf16[64,1,2,128,128]{4,3,2,1,0:T(8,128)(2,1)S(1)} %bitcast_select_fusion), channel_id=1, replica_groups=mesh['rows'=64,'grp'=4] {'rows'}, dimensions={0} | all-to-all | bytes 8388608 | tf_op jit(solution)/shard_map/all_to_all | solution.py:64
  122.5 0.6 copy-done.3
  123.2 0.2 select_reduce_fusion.1
  123.7 0.8 gather_fusion.1
  124.5 0.6 gather_fusion
  125.6 0.2 copy.48
  125.7 0.3 select_reduce_fusion
  126.4 0.6 gather_fusion.2
  128.0 4.1 convolution_bitcast_fusion.1
  132.1 7.3 %copy.52 = f32[8,3,2,2,128,128]{5,4,3,2,1,0:T(8,128)} copy(f32[8,3,2,2,128,128]{4,5,2,3,1,0:T(8,128)} %convolution_bitcast_fusion.1) | data formatting | bytes 12582912 | tf_op jit(solution)/shard_map/while/body/eval_jaxpr/riaq,rkjac->rkijqc/transpose | solution.py:18
  139.6 6.8 %broadcast_in_dim.99 = f32[2,98,128,128]{3,2,1,0:T(8,128)} broadcast(f32[]{:T(128)} %constant.44.clone.1), dimensions={} | broadcast | bytes 12845060 | tf_op jit(solution)/shard_map/broadcast_in_dim | solution.py:54
  146.3 20.2 %scatter_fusion = f32[2,98,128,128]{3,2,1,0:T(8,128)} fusion(f32[2,98,128,128]{3,2,1,0:T(8,128)} %broadcast_in_dim.99, s32[96]{0:T(128)S(1)} %reshape.181, f32[96,128,128]{2,1,0:T(8,128)} %bitcast.64), kind=kCustom, calls=%fused_computation.5 | custom fusion | flops 1572864 | bytes 18875136 | tf_op jit(solution)/shard_map/while/body/eval_jaxpr/scatter-add | solution.py:24
  166.5 110.5 %all-gather.2.cloned.1.call-done = bf16[64,4,2,128,128]{4,3,2,1,0:T(8,128)(2,1)} async-done(((bf16[64,1,2,128,128]{4,3,2,1,0:T(8,128)(2,1)}), bf16[64,4,2,128,128]{4,3,2,1,0:T(8,128)(2,1)}) %all-gather.2.cloned.1.call-update) | async-done | bytes 16777232 | tf_op jit(solution)/shard_map/all_gather | solution.py:65
  276.9 6.6 %gather_fusion.4 = bf16[24,2,128,128]{3,2,1,0:T(8,128)(2,1)S(1)} fusion(bf16[256,2,128,128]{3,2,1,0:T(8,128)(2,1)} %bitcast.69, s32[1024]{0:T(1024)S(1)} %pad_clamp_fusion.1), kind=kCustom, calls=%fused_computation.4 | custom fusion | bytes 3145824 | tf_op jit(solution)/shard_map/gather | solution.py:70
  283.5 5.2 %convolution_bitcast_fusion = f32[8,3,2,2,128,128]{4,5,2,3,1,0:T(8,128)} fusion(bf16[8,3,2,128,128]{4,3,2,1,0:T(8,128)(2,1)S(1)} %bitcast.67, bf16[8,3,128,128]{3,2,1,0:T(8,128)(2,1)} %param.11, bf16[8,2,128,128]{3,2,1,0:T(8,128)(2,1)S(1)} %copy-done.2), kind=kOutput, calls=%fused_computation.8 | convolution fusion | flops 604766208 | bytes 9175040 | tf_op jit(solution)/shard_map/while/body/eval_jaxpr/riaq,rkjac->rkijqc/dot_general | solution.py:18
  288.8 6.6 %copy.60 = f32[8,3,2,2,128,128]{5,4,3,2,1,0:T(8,128)} copy(f32[8,3,2,2,128,128]{4,5,2,3,1,0:T(8,128)} %convolution_bitcast_fusion) | data formatting | bytes 12582912 | tf_op jit(solution)/shard_map/while/body/eval_jaxpr/riaq,rkjac->rkijqc/transpose | solution.py:18
  295.4 20.7 %scatter_fusion.1 = f32[2,98,128,128]{3,2,1,0:T(8,128)} fusion(f32[2,98,128,128]{3,2,1,0:T(8,128)} %scatter_fusion, s32[96]{0:T(128)S(1)} %reshape.187, f32[96,128,128]{2,1,0:T(8,128)} %bitcast.65), kind=kCustom, calls=%fused_computation.6 | custom fusion | flops 1572864 | bytes 18875136 | tf_op jit(solution)/shard_map/while/body/eval_jaxpr/scatter-add | solution.py:24
  316.1 120.2 %reduce-scatter.2.cloned.1.call-done = f32[2,98,32,128]{3,2,1,0:T(8,128)} async-done(((f32[2,98,128,128]{3,2,1,0:T(8,128)}), f32[2,98,32,128]{3,2,1,0:T(8,128)}) %reduce-scatter.2.cloned.1.call-update) | async-done | bytes 3211280 | tf_op jit(solution)/shard_map/reduce_scatter | solution.py:71
  436.3 3.4 convert_element_type.21
  (53 shorter events, 2.4 us)
Async XLA Ops:
  6.5 121.5 %copy-start = (bf16[8,3,128,128]{3,2,1,0:T(8,128)(2,1)S(1)}, bf16[8,3,128,128]{3,2,1,0:T(8,128)(2,1)}, u32[]{:S(2)}) copy-start(bf16[8,3,128,128]{3,2,1,0:T(8,128)(2,1)} %param.9) | copy-start | bytes 2359300
  6.5 270.4 %all-gather.2.cloned.1.call-start = ((), (), s32[]{:S(2)}) async-start(), calls=%async_computation.2 | async-start | bytes 20971520 | tf_op jit(solution)/shard_map/all_gather | solution.py:65
  122.4 0.7 copy-start.3
  122.4 0.8 copy-start.5
  122.4 1.1 copy-start.6
  122.4 1.2 copy-start.2
  122.4 3.3 copy-start.4
  122.5 3.8 copy-start.7
  122.5 313.8 %reduce-scatter.2.cloned.1.call-start = ((), (), s32[]{:S(2)}) async-start(), calls=%async_computation.3 | async-start | bytes 16056320 | tf_op jit(solution)/shard_map/reduce_scatter | solution.py:71
  316.1 123.6 %copy-start.1 = (bf16[8,3,128,128]{3,2,1,0:T(8,128)(2,1)S(1)}, bf16[8,3,128,128]{3,2,1,0:T(8,128)(2,1)}, u32[]{:S(2)}) copy-start(bf16[8,3,128,128]{3,2,1,0:T(8,128)(2,1)} %param.9) | copy-start | bytes 2359300
Sparse Core Ops, SparseCore 0:
  122.6 154.2 all-gather.1
  316.2 120.0 reduce-scatter.1
where the time goes:
time: 447 us
  waiting for transfers between devices  231 us (52%)
  blocking collectives  108 us (24%)
  other arithmetic  49.1 us (11%)
  local copies, waits for them, and re-layouts  36.2 us (8%)
  between operations  13.6 us (3%)
  matrix products  9.33 us (2%)
    reduce_scatter x1, waiting for transfers between devices, per_device(): summed = lax.psum_scatter(running, 'grp', scatter_dimension=2, tiled=True)  120 us
    all_gather x1, waiting for transfers between devices, per_device(): arrived = lax.all_gather(arrived, 'grp', axis=1, tiled=True)  110 us
    all_to_all x1, blocking collectives, per_device(): lax.all_to_all(outgoing, 'rows', split_axis=0, concat_axis=0, tiled=True)  108 us
    scatter-add x2, other arithmetic, galerkin_terms(): return running.at[rows_idx, cols_idx].add(galerkin_part)  40.9 us
    transpose x2, local copies, waits for them, and re-layouts, galerkin_terms(): jnp.einsum('riaq,rkjac->rkijqc', left_tiles, products_ab, preferred_eleme...  13.9 us
    dot_general x2, matrix products, galerkin_terms(): jnp.einsum('riaq,rkjac->rkijqc', left_tiles, products_ab, preferred_eleme...  9.33 us
  transfers between devices with their start and end apart: 2, of which 2 were waited for; matrix products, arithmetic and copies ran while one was open for 10% of the time, Pallas kernels for 0%

commit v1 on v0

v1 whole, which is shorter than its diff:
```python
import functools

import jax
import jax.numpy as jnp
from jax import lax
from jax.experimental import pallas as pl
from jax.experimental.pallas import tpu as pltpu
from jax.sharding import PartitionSpec as P

CR1 = 2
T = 128
H = T // 2


def ordered_tiles(prolong, aggregate):
    first = (aggregate[:, 0] == 0)[:, None, None]
    zero = jnp.where(first, prolong[:, 0], prolong[:, 1])
    one = jnp.where(first, prolong[:, 1], prolong[:, 0])
    return jnp.concatenate([zero, one], axis=-1)


def left_kernel(a_ref, p_ref, l_ref):
    left = p_ref[0].T
    groups, _, per, _, _ = a_ref.shape
    for g in range(groups):
        for k in range(per):
            l_ref[0, g * per + k] = jnp.dot(
                left, a_ref[g, 0, k], preferred_element_type=jnp.float32
            ).astype(l_ref.dtype)


def left_factors(a_all, ordered):
    groups, rows, per, _, _ = a_all.shape
    count = groups * per
    return pl.pallas_call(
        left_kernel,
        grid=(rows,),
        in_specs=[
            pl.BlockSpec((groups, 1, per, T, T), lambda i: (0, i, 0, 0, 0)),
            pl.BlockSpec((1, T, 2 * T), lambda i: (i, 0, 0)),
        ],
        out_specs=pl.BlockSpec((1, count, 2 * T, T), lambda i: (i, 0, 0, 0)),
        out_shape=jax.ShapeDtypeStruct((rows, count, 2 * T, T), jnp.bfloat16),
        cost_estimate=pl.CostEstimate(
            flops=rows * count * 4 * T**3, bytes_accessed=rows * count * 6 * T * T, transcendentals=0
        ),
        name="left_factors",
    )(a_all, ordered)


def diag_kernel(cols_ref, a_ref, p_ref, d_ref):
    rows, per, _, _ = a_ref.shape

    def row(i, _):
        left = p_ref[i].T
        for k in range(per):
            part = jnp.dot(left, a_ref[i, k], preferred_element_type=jnp.float32)
            d_ref[...] += jnp.dot(
                part.astype(jnp.bfloat16), p_ref[cols_ref[i, k]], preferred_element_type=jnp.float32
            )
        return 0

    d_ref[...] = jnp.zeros_like(d_ref)
    lax.fori_loop(0, rows, row, 0)


def diag_terms(a_diag, diag_cols, ordered):
    rows, per, _, _ = a_diag.shape
    return pl.pallas_call(
        diag_kernel,
        in_specs=[
            pl.BlockSpec(memory_space=pltpu.SMEM),
            pl.BlockSpec(memory_space=pltpu.VMEM),
            pl.BlockSpec(memory_space=pltpu.VMEM),
        ],
        out_specs=pl.BlockSpec(memory_space=pltpu.VMEM),
        out_shape=jax.ShapeDtypeStruct((2 * T, 2 * T), jnp.float32),
        cost_estimate=pl.CostEstimate(
            flops=rows * per * 12 * T**3, bytes_accessed=rows * per * 2 * T * T, transcendentals=0
        ),
        name="diag_terms",
    )(diag_cols, a_diag, ordered)


def offd_kernel(node_ref, pair_ref, odd_ref, l_ref, gath_ref, out_ref, rbuf, acc, sem):
    i = pl.program_id(0)
    rows = pl.num_programs(0)
    count = l_ref.shape[1]

    @pl.when(i == 0)
    def _():
        def fetch(t, _):
            pltpu.make_async_copy(
                gath_ref.at[pair_ref[t]], rbuf.at[t // count, t % count], sem.at[t // count]
            ).start()
            return 0

        lax.fori_loop(0, rows * count, fetch, 0)
        acc[...] = jnp.zeros_like(acc)

    pltpu.make_async_copy(gath_ref.at[pl.ds(0, count)], rbuf.at[i], sem.at[i]).wait()
    high = lax.broadcasted_iota(jnp.int32, (T, T), 1) >= H
    for k in range(count):
        t = i * count + k
        odd = odd_ref[t] == 1
        y = jnp.dot(l_ref[0, k], rbuf[i, k], preferred_element_type=jnp.float32)
        kept = jnp.where(odd, y[T:], y[:T])
        moved = jnp.where(odd, y[:T], y[T:])
        acc[node_ref[t]] += jnp.where(high == odd, kept, pltpu.roll(moved, H, 1))

    @pl.when(i == rows - 1)
    def _():
        quarter = out_ref.shape[2]
        for g in range(out_ref.shape[0]):
            out_ref[g] = acc[:, g * quarter : (g + 1) * quarter, :].astype(out_ref.dtype)


def offd_terms(nodes, pairs, odds, left, gathered, groups):
    rows, count, _, _ = left.shape
    total = gathered.shape[0]
    node_count = total // 4
    quarter = T // groups
    return pl.pallas_call(
        offd_kernel,
        grid_spec=pltpu.PrefetchScalarGridSpec(
            num_scalar_prefetch=3,
            grid=(rows,),
            in_specs=[
                pl.BlockSpec((1, count, 2 * T, T), lambda i, *_: (i, 0, 0, 0)),
                pl.BlockSpec(memory_space=pl.ANY),
            ],
            out_specs=pl.BlockSpec((groups, node_count, quarter, T), lambda i, *_: (0, 0, 0, 0)),
            scratch_shapes=[
                pltpu.VMEM((rows, count, T, T), jnp.bfloat16),
                pltpu.VMEM((node_count, T, T), jnp.float32),
                pltpu.SemaphoreType.DMA((rows,)),
            ],
        ),
        out_shape=jax.ShapeDtypeStruct((groups, node_count, quarter, T), jnp.bfloat16),
        compiler_params=pltpu.CompilerParams(vmem_limit_bytes=40 << 20),
        cost_estimate=pl.CostEstimate(
            flops=rows * count * 4 * T**3, bytes_accessed=rows * count * 6 * T * T, transcendentals=0
        ),
        name="offd_terms",
    )(nodes, pairs, odds, left, gathered)


def place_kernel(map_ref, me_ref, x_ref, d_ref, out_ref):
    slots = out_ref.shape[1]
    quarter = out_ref.shape[2]
    high = lax.broadcasted_iota(jnp.int32, (quarter, T), 1) >= H
    me = me_ref[0]

    def place(m, _):
        gid = map_ref[m]
        node, agg = gid // CR1, gid % CR1
        own = node == me
        left = x_ref[2 * agg, node].astype(jnp.float32)
        right = x_ref[2 * agg + 1, node].astype(jnp.float32)
        top = jnp.where(high, pltpu.roll(right, H, 1), left)
        low = jnp.where(high, right, pltpu.roll(left, H, 1))
        out_ref[0, m] = jnp.where(own, d_ref[0, agg], top).astype(out_ref.dtype)
        out_ref[1, m] = jnp.where(own, d_ref[1, agg], low).astype(out_ref.dtype)
        return 0

    lax.fori_loop(0, slots, place, 0, unroll=2)


def place_slots(col_map, me, arrived, own):
    slots = col_map.shape[0]
    quarter = arrived.shape[2]
    vmem = pl.BlockSpec(memory_space=pltpu.VMEM)
    smem = pl.BlockSpec(memory_space=pltpu.SMEM)
    return pl.pallas_call(
        place_kernel,
        in_specs=[smem, smem, vmem, vmem],
        out_specs=vmem,
        out_shape=jax.ShapeDtypeStruct((CR1, slots, quarter, T), jnp.bfloat16),
        compiler_params=pltpu.CompilerParams(vmem_limit_bytes=16 << 20),
        name="place_slots",
    )(col_map, me, arrived, own)


def per_device(
    a_diag, diag_cols, a_offd, offd_cols, prolong, aggregate, send_rows, ghost_agg, coarse_map
):
    groups = lax.axis_size("grp")
    me = lax.axis_index("rows")
    grp = lax.axis_index("grp")
    agg, half = grp // 2, grp % 2
    rows = prolong.shape[0]

    mine = jnp.where((aggregate[:, 0] == agg)[:, None, None], prolong[:, 0], prolong[:, 1])
    mine = jnp.where(half == 0, mine[..., :H], mine[..., H:])
    mine = jnp.concatenate([mine[0::2], mine[1::2]], axis=-1)
    gathered = lax.all_gather(mine, "rows", axis=0, tiled=True)
    a_all = lax.all_gather(a_offd, "grp", axis=0, tiled=False)
    rows_all = lax.all_gather(send_rows, "rows", axis=0, tiled=True)
    cols_all = lax.all_gather(offd_cols, "grp", axis=1, tiled=True)

    ordered = ordered_tiles(prolong, aggregate)
    partial = diag_terms(a_diag, diag_cols, ordered)
    partial = jnp.transpose(partial.reshape(CR1, T, CR1, T), (0, 2, 1, 3))
    own = lax.psum_scatter(partial, "grp", scatter_dimension=2, tiled=True)

    left = left_factors(a_all, ordered)

    cols = cols_all.reshape(-1)
    slots = send_rows.shape[2]
    nodes = cols // slots
    from_me = lax.dynamic_index_in_dim(rows_all, me, 1, keepdims=False).reshape(-1)
    rid = jnp.sum(
        jnp.where(cols[:, None] == jnp.arange(from_me.shape[0], dtype=jnp.int32), from_me, 0), axis=1
    )
    pairs = nodes * (rows // 2) + rid // 2
    offd = offd_terms(nodes, pairs, rid % 2, left, gathered, groups)
    arrived = lax.all_to_all(offd, "grp", split_axis=0, concat_axis=0, tiled=True)
    return place_slots(coarse_map[0], me.reshape(1), arrived, own)


def solution(mesh):
    in_specs = (
        P("rows", "grp", None, None),
        P("rows", "grp"),
        P("rows", "grp", None, None),
        P("rows", "grp"),
        P("rows", None, None, None),
        P("rows", None),
        P("rows", None, None),
        P("rows", None, None, None),
        P("rows", None),
    )
    out_specs = P("rows", None, "grp", None)
    return jax.shard_map(
        per_device, mesh=mesh, in_specs=in_specs, out_specs=out_specs, check_vma=False
    )
```

time: 447 us -> 201 us (0.45)
  waiting for transfers between devices: 231 us -> 80.6 us
  other arithmetic: 49.1 us -> 3.79 us
  blocking collectives: 108 us -> 62.8 us
  Pallas kernels: 0 us -> 28.6 us
  local copies, waits for them, and re-layouts: 36.2 us -> 7.66 us
  matrix products: 9.33 us -> 0 us
    all_to_all x1 -> x0, blocking collectives: 108 us -> none  [per_device(): lax.all_to_all(outgoing, 'rows', split_axis=0, concat_axis=0, tiled=True)]
    reduce_scatter x1, waiting for transfers between devices: 120 us -> 21.9 us  [per_device(): own = lax.psum_scatter(partial, 'grp', scatter_dimension=2, tiled=True)]
    all_gather x0 -> x2, blocking collectives: none -> 62.8 us  [the longest x1 54.3 us: per_device(): rows_all = lax.all_gather(send_rows, 'rows', axis=0, tiled=True)]
    all_gather x1 -> x2, waiting for transfers between devices: 110 us -> 58 us  [the longest x1 58 us: per_device(): gathered = lax.all_gather(mine, 'rows', axis=0, tiled=True)]
    scatter-add x2 -> x0, other arithmetic: 40.9 us -> none  [galerkin_terms(): return running.at[rows_idx, cols_idx].add(galerkin_part)]
    pallas_call x0 -> x4, Pallas kernels: none -> 28.6 us  [the longest x1 8.08 us: left_factors(): pl.pallas_call(left_kernel, grid=(rows,), in_specs=[pl.BlockSpec((groups,...]
    transpose x2 -> x0, local copies, waits for them, and re-layouts: 13.9 us -> none  [galerkin_terms(): jnp.einsum('riaq,rkjac->rkijqc', left_tiles, products_ab, preferred_eleme...]
    gather x11 -> x0, local copies, waits for them, and re-layouts: 12.2 us -> none  [the longest x1 6.62 us: per_device(): ghosts[offd_cols]]
  transfers between devices with their start and end apart: 2 -> 4, of which waited for: 2 -> 2; matrix products, arithmetic and copies ran while one was open for 10% -> 4% of each run, Pallas kernels for 0% -> 7%
where the time goes in v1:
time: 201 us
  waiting for transfers between devices  80.6 us (40%)
  blocking collectives  62.8 us (31%)
  Pallas kernels  28.6 us (14%)
  between operations  13.2 us (7%)
  local copies, waits for them, and re-layouts  7.66 us (4%)
  starting transfers between devices  4.02 us (2%)
  other arithmetic  3.79 us (2%)
    all_gather x1, waiting for transfers between devices, per_device(): gathered = lax.all_gather(mine, 'rows', axis=0, tiled=True)  58 us
    all_gather x1, blocking collectives, per_device(): rows_all = lax.all_gather(send_rows, 'rows', axis=0, tiled=True)  54.3 us
    reduce_scatter x1, waiting for transfers between devices, per_device(): own = lax.psum_scatter(partial, 'grp', scatter_dimension=2, tiled=True)  21.9 us
    all_gather x1, blocking collectives, per_device(): cols_all = lax.all_gather(offd_cols, 'grp', axis=1, tiled=True)  8.43 us
    pallas_call x1, Pallas kernels, left_factors(): pl.pallas_call(left_kernel, grid=(rows,), in_specs=[pl.BlockSpec((groups,...  8.08 us
    pallas_call x1, Pallas kernels, offd_terms(): pl.pallas_call(offd_kernel, grid_spec=pltpu.PrefetchScalarGridSpec(num_sc...  7.64 us
    pallas_call x1, Pallas kernels, diag_terms(): pl.pallas_call(diag_kernel, in_specs=[pl.BlockSpec(memory_space=pltpu.SME...  6.79 us
    pallas_call x1, Pallas kernels, place_slots(): pl.pallas_call(place_kernel, in_specs=[smem, smem, vmem, vmem], out_specs...  6.06 us
  transfers between devices with their start and end apart: 4, of which 2 were waited for; matrix products, arithmetic and copies ran while one was open for 4% of the time, Pallas kernels for 7%

profile of v1, /device:TPU:1, one launch (start us, length us, event | category | flops | bytes accessed | tf_op | source)
XLA Modules:
  0.0 200.6 jit_solution(17355950140769981246)
XLA Ops:
  6.5 0.7 all-gather.7.cloned.1.call-update
  7.3 0.7 compare_bitcast_fusion
  8.0 1.1 bitcast_select_fusion.2
  9.2 0.1 slice_select_fusion
  9.3 0.8 pad_maximum_fusion.1
  10.1 54.3 %all_gather.16 = s32[64,64,4]{1,2,0:T(4,128)S(1)} all-gather(s32[1,64,4]{1,2,0:T(4,128)S(1)} %copy-done.3), channel_id=1, replica_groups=mesh['rows'=64,'grp'=4] {'rows'}, dimensions={0}, use_global_device_ids=true | all-gather | bytes 66560 | tf_op jit(solution)/shard_map/all_gather | solution.py:198
  64.5 1.2 dynamic-slice_reduce_fusion
  65.7 0.1 reshape.30
  65.8 8.4 %all-gather.1 = s32[4,3,8]{2,1,0:T(4,128)S(1)} all-gather(s32[1,3,8]{2,1,0:T(4,128)S(1)} %bitcast.30), channel_id=1, replica_groups=mesh['rows'=64,'grp'=4] {'grp'}, dimensions={0}, use_global_device_ids=true | all-gather | bytes 480 | tf_op jit(solution)/shard_map/all_gather | solution.py:199
  74.3 0.1 copy.23
  74.4 0.2 select_reduce_fusion
  74.6 0.9 pad_maximum_fusion.p_ref
  75.5 8.1 %left_factors.1.l_ref = bf16[8,12,256,128]{3,2,1,0:T(8,128)(2,1)} custom-call(bf16[4,8,3,128,128]{4,3,2,1,0:T(8,128)(2,1)} %bitcast.27, bf16[8,128,256]{2,1,0:T(8,128)(2,1)} %pad_maximum_fusion.p_ref), custom_call_target="tpu_custom_call" | custom-call | flops 805306368 | bytes 9437184 | tf_op jit(solution)/shard_map/left_factors/pallas_call | solution.py:35
  83.6 58.0 %all-gather.5.cloned.1.call-done.gath_ref = bf16[256,128,128]{2,1,0:T(8,128)(2,1)} async-done(((bf16[4,128,128]{2,1,0:T(8,128)(2,1)}), bf16[256,128,128]{2,1,0:T(8,128)(2,1)}) %all-gather.5.cloned.1.call-update) | async-done | bytes 8388624 | tf_op jit(solution)/shard_map/all_gather | solution.py:196
  141.6 2.8 %copy-done = bf16[8,12,256,128]{3,2,1,0:T(8,128)(2,1)S(1)} copy-done((bf16[8,12,256,128]{3,2,1,0:T(8,128)(2,1)S(1)}, bf16[8,12,256,128]{3,2,1,0:T(8,128)(2,1)}, u32[]{:S(2)}) %copy-start) | copy-done | bytes 6291480
  144.4 7.6 %offd_terms.1 = bf16[4,64,32,128]{3,2,1,0:T(8,128)(2,1)} custom-call(s32[96]{0:T(128)S(1)} %get-tuple-element.6.node_ref, s32[96]{0:T(128)S(1)} %get-tuple-element.5.pair_ref, s32[96]{0:T(128)S(1)} %get-tuple-element.14.odd_ref, bf16[8,12,256,128]{3,2,1,0:T(8,128)(2,1)S(1)} %copy-done, bf16[256,128,128]{2,1,0:T(8,128)(2,1)} %all-gather.5.cloned.1.call-done.gath_ref), custom_call_target="tpu_custom_call" | custom-call | flops 805306368 | bytes 9437184 | tf_op jit(solution)/shard_map/offd_terms/pallas_call | solution.py:123
  152.0 4.0 %all-to-all-start = ((bf16[4,64,32,128]{3,2,1,0:T(8,128)(2,1)}), bf16[4,64,32,128]{3,2,1,0:T(8,128)(2,1)S(1)}, u32[]{:S(2)}, u32[]{:S(2)}) async-start(bf16[4,64,32,128]{3,2,1,0:T(8,128)(2,1)} %offd_terms.1), calls=%async_computation | async-start | bytes 4194304 | tf_op jit(solution)/shard_map/all_to_all | solution.py:217
  156.0 0.7 copy.26.cols_ref
  156.7 6.8 %diag_terms.1 = f32[256,256]{1,0:T(8,128)} custom-call(s32[8,3]{1,0:T(8,128)} %copy.26.cols_ref, bf16[8,3,128,128]{3,2,1,0:T(8,128)(2,1)} %a_ref.1, bf16[8,128,256]{2,1,0:T(8,128)(2,1)} %pad_maximum_fusion.p_ref), custom_call_target="tpu_custom_call" | custom-call | flops 603979776 | bytes 786432 | tf_op jit(solution)/shard_map/diag_terms/pallas_call | solution.py:69
  163.5 1.1 reshape.31
  164.6 0.7 copy.31
  165.3 21.9 %reduce-scatter.2.cloned.1.call-done.d_ref = f32[2,2,32,128]{3,2,1,0:T(8,128)} async-done(((f32[2,2,128,128]{3,2,1,0:T(8,128)}), f32[2,2,32,128]{3,2,1,0:T(8,128)}) %reduce-scatter.2.cloned.1.call-update) | async-done | bytes 65552 | tf_op jit(solution)/shard_map/reduce_scatter | solution.py:204
  187.2 0.8 copy-done.1
  188.1 6.1 %place_slots.1 = bf16[2,98,32,128]{3,2,1,0:T(8,128)(2,1)} custom-call(s32[98]{0:T(128)S(1)} %bitcast.26, s32[1]{0:T(128)} %bitcast.1.me_ref, bf16[4,64,32,128]{3,2,1,0:T(8,128)(2,1)S(1)} %all-to-all-done.x_ref, f32[2,2,32,128]{3,2,1,0:T(8,128)S(1)} %copy-done.1), custom_call_target="tpu_custom_call" | custom-call | tf_op jit(solution)/shard_map/place_slots/pallas_call | solution.py:174
  (21 shorter events, 0.2 us)
Async XLA Ops:
  6.5 3.6 %copy-start.3 = (s32[1,64,4]{1,2,0:T(4,128)S(1)}, s32[1,64,4]{1,2,0:T(4,128)}, u32[]{:S(2)}) copy-start(s32[1,64,4]{1,2,0:T(4,128)} %param.15) | copy-start | bytes 3076
  6.5 59.3 %copy-start.4 = (s32[8,3]{0,1:T(4,128)S(1)}, s32[8,3]{0,1:T(4,128)}, u32[]{:S(2)}) copy-start(s32[8,3]{0,1:T(4,128)} %param.12) | copy-start | bytes 292
  6.5 69.0 %all-gather.7.cloned.1.call-start = ((), (), s32[]{:S(2)}) async-start(), calls=%async_computation.4 | async-start | bytes 3932160 | tf_op jit(solution)/shard_map/all_gather | solution.py:197
  7.3 134.3 %all-gather.5.cloned.1.call-start = ((), (), s32[]{:S(2)}) async-start(), calls=%async_computation.2 | async-start | bytes 8519680 | tf_op jit(solution)/shard_map/all_gather | solution.py:196
  141.6 2.8 %copy-start = (bf16[8,12,256,128]{3,2,1,0:T(8,128)(2,1)S(1)}, bf16[8,12,256,128]{3,2,1,0:T(8,128)(2,1)}, u32[]{:S(2)}) copy-start(bf16[8,12,256,128]{3,2,1,0:T(8,128)(2,1)} %left_factors.1.l_ref) | copy-start | bytes 18874372
  152.0 4.0 %copy-start.5 = (s32[8,3]{0,1:T(4,128)S(1)}, s32[8,3]{0,1:T(4,128)}, u32[]{:S(2)}) copy-start(s32[8,3]{0,1:T(4,128)} %param.10) | copy-start | bytes 292
  152.0 35.2 %copy-start.2 = (s32[1,98]{1,0:T(1,128)S(1)}, s32[1,98]{1,0:T(1,128)}, u32[]{:S(2)}) copy-start(s32[1,98]{1,0:T(1,128)} %param.16) | copy-start | bytes 1180
  152.0 35.2 %all-to-all-start = ((bf16[4,64,32,128]{3,2,1,0:T(8,128)(2,1)}), bf16[4,64,32,128]{3,2,1,0:T(8,128)(2,1)S(1)}, u32[]{:S(2)}, u32[]{:S(2)}) async-start(bf16[4,64,32,128]{3,2,1,0:T(8,128)(2,1)} %offd_terms.1), calls=%async_computation | async-start | bytes 4194304 | tf_op jit(solution)/shard_map/all_to_all | solution.py:217
  156.0 31.2 %reduce-scatter.2.cloned.1.call-start = ((), (), s32[]{:S(2)}) async-start(), calls=%async_computation.3 | async-start | bytes 327680 | tf_op jit(solution)/shard_map/reduce_scatter | solution.py:204
  187.2 0.8 copy-start.1
Sparse Core Ops, SparseCore 0:
  9.2 45.8 all-gather.6
  57.8 83.6 all-gather.4
  165.4 21.7 reduce-scatter.1

commit v2 on v1

v2 whole, which is shorter than its diff:
```python
import functools

import jax
import jax.numpy as jnp
from jax import lax
from jax.experimental import pallas as pl
from jax.experimental.pallas import tpu as pltpu
from jax.sharding import PartitionSpec as P

CR1 = 2
T = 128
H = T // 2


ROWS = 528
ZR = 320
NZ, NY = 8, 4
MESH = pl.DeviceIdType.MESH
PARTS = {"z": (0, ZR), "za": (0, ZR // 2), "zb": (ZR // 2, ZR // 2),
         "y": (ZR, ROWS - ZR), "ya": (ZR, 112), "yb": (ZR + 112, ROWS - ZR - 112)}
DZ = (0, 1, -1, 2, -2, 3, -3, 4)
LATE_UP = (0, 1, 2, 3)


def flood_plan():
    plan = {}

    def add(name, link, there, here, part, after):
        plan[name] = (link, there, here, part, tuple(after))

    for sign, link in ((1, "z+"), (-1, "z-")):
        for d in range(1, 5):
            part = "z" if d < 4 else ("za" if sign == 1 else "zb")
            after = [] if d == 1 else [("Z", sign * (d - 1))]
            here = sign * d if d < 4 else 4
            name = ("Z", here) if d < 4 else ("Z", 4, sign)
            add(name, link, (sign * (d - 1), 0), (here, 0), part, after)
    for e in DZ:
        have = [] if e == 0 else ([("Z", e)] if e != 4 else [("Z", 4, 1), ("Z", 4, -1)])
        for sign, link in ((1, "y+"), (-1, "y-")):
            add(("ZY", e, sign), link, (e, 0), (e, sign), "z", have)
        sign = 1 if e in LATE_UP else -1
        add(("ZY", e, 2), "y+" if sign == 1 else "y-", (e, sign), (e, 2), "z", [("ZY", e, sign)])
    for sign, link in ((1, "y+"), (-1, "y-")):
        add(("Y", sign), link, (0, 0), (0, sign), "y", [])
        add(("Y", 2, sign), link, (0, sign), (0, 2), "ya" if sign == 1 else "yb", [("Y", sign)])
    for sign, link in ((1, "z+"), (-1, "z-")):
        for d in range(1, 5):
            for dy in (0, 1, -1, 2):
                if d == 4 and (dy in (0, 1)) != (sign == 1):
                    continue
                if d > 1:
                    after = [("YZ", sign * (d - 1), dy)]
                elif dy == 0:
                    after = []
                else:
                    after = [("Y", dy)] if dy != 2 else [("Y", 2, 1), ("Y", 2, -1)]
                here = sign * d if d < 4 else 4
                add(("YZ", here, dy), link, (sign * (d - 1), dy), (here, dy), "y", after)
    return plan


def flood_order(plan):
    free = {}
    arrive, waiting = {}, dict(plan)
    rank = {"Y": 0, "Z": 1, "YZ": 2, "ZY": 3}
    while len(arrive) < len(plan):
        best = None
        for name, (link, _, _, part, after) in waiting.items():
            if any(a not in arrive for a in after):
                continue
            start = max([arrive[a] for a in after] + [free.get(link, 0.0)])
            key = (start, rank[name[0]], abs(name[1]), str(name))
            if best is None or key < best[0]:
                best = (key, name, start, link, part)
        _, name, start, link, part = best
        end = start + PARTS[part][1] * 256 / 50e3
        free[link] = end
        arrive[name] = end + 1.5
        del waiting[name]
    return arrive


def gather_kernel(
    agg_ref, dcols_ref, ocols_ref, srows_ref, p_ref, ad_ref, ao_ref,
    gath, left_out, own_ref, tbl_ref, cols_ref,
    mine, ordered, left_t, a_all, left, dacc, drecv, ctab, ext,
    ssem, rsem, xs_sem, xr_sem, lsem,
):
    me = lax.axis_index("rows")
    x = lax.axis_index("grp")
    core = lax.rem(me, 2)
    y = lax.rem(me // 2, NY)
    z = me // (2 * NY)

    def row_of(zz, yy, cc):
        return (zz * NY + yy) * 2 + cc

    up_z, dn_z = lax.rem(z + 1, NZ), lax.rem(z + NZ - 1, NZ)
    up_y, dn_y = lax.rem(y + 1, NY), lax.rem(y + NY - 1, NY)
    xat = [lax.rem(x + d, 4) for d in range(4)]
    link_to = {
        "z+": (row_of(up_z, y, core), x),
        "z-": (row_of(dn_z, y, core), x),
        "y+": (row_of(z, up_y, core), x),
        "y-": (row_of(z, dn_y, core), x),
        "core": (row_of(z, y, 1 - core), x),
        1: (me, xat[1]),
        2: (me, xat[2]),
        3: (me, xat[3]),
    }
    barrier = pltpu.get_barrier_semaphore()
    for device in link_to.values():
        pl.semaphore_signal(barrier, inc=1, device_id=device, device_id_type=MESH)
    pl.semaphore_wait(barrier, len(link_to))

    sends = []

    def remote(src, dst, s, r, device):
        return pltpu.make_async_remote_copy(
            src_ref=src, dst_ref=dst, send_sem=s, recv_sem=r, device_id=device, device_id_type=MESH
        )

    half = ao_ref.shape[0] // 2
    first, second = pl.ds(0, half), pl.ds(half, half)
    a_plan = {
        ("r", 0): (0, 1, first, 1), ("r", 1): (0, 1, second, 1), ("r", 2): (1, 2, first, 1),
        ("l", 1): (0, 3, second, 3), ("l", 0): (0, 3, first, 3), ("l", 2): (3, 2, second, 3),
    }
    a_index = {name: i for i, name in enumerate(a_plan)}

    def a_copy(name, sending):
        src_slot, dst_slot, part, to = a_plan[name]
        dst = a_all.at[dst_slot, part]
        src = (ao_ref if src_slot == 0 else a_all.at[src_slot]).at[part] if sending else dst
        i = a_index[name]
        return remote(src, dst, xs_sem.at[i], xr_sem.at[i], link_to[to])

    def a_send(name):
        copy = a_copy(name, True)
        copy.start()
        sends.append(copy)

    for name in (("r", 0), ("l", 1), ("r", 1), ("l", 0)):
        a_send(name)

    def c_copy(d, sending):
        src = ctab.at[0]
        return remote(src, ctab.at[d], xs_sem.at[5 + d], xr_sem.at[5 + d], link_to[d])

    ctab[0, :, 0 : ocols_ref.shape[1]] = ocols_ref[...]
    for d in (1, 2, 3):
        copy = c_copy(d, True)
        copy.start()
        sends.append(copy)

    agg, side = x // 2, lax.rem(x, 2)
    high = lax.broadcasted_iota(jnp.int32, (T, T), 1) >= H
    rows = p_ref.shape[0]
    for p in range(rows // 2):
        even = jnp.where(agg_ref[2 * p, 0] == agg, p_ref[2 * p, 0], p_ref[2 * p, 1]).astype(jnp.float32)
        odd = jnp.where(agg_ref[2 * p + 1, 0] == agg, p_ref[2 * p + 1, 0], p_ref[2 * p + 1, 1])
        odd = odd.astype(jnp.float32)
        kept = jnp.where(side == 0, even, odd)
        moved = pltpu.roll(jnp.where(side == 0, odd, even), H, 1)
        pair = jnp.where(high == (side == 1), kept, moved)
        mine[p * T : (p + 1) * T, :] = pair.astype(mine.dtype)
    tail = jnp.concatenate(
        [srows_ref[...].astype(jnp.float32), jnp.zeros((14, T), jnp.float32)], axis=0
    )
    mine[4 * T :, :] = tail.astype(mine.dtype)

    plan = flood_plan()
    names = sorted(plan, key=str)
    index = {name: i for i, name in enumerate(names)}
    sib = {}

    def block(offset, rows_at, plane=None):
        dz, dy = offset
        return gath.at[
            core if plane is None else plane,
            lax.rem(z + (NZ - dz), NZ), lax.rem(y + (NY - dy), NY), pl.ds(*rows_at)
        ]

    def f_copy(name, sending):
        link, there, here, part, _ = plan[name]
        at = PARTS[part]
        dst = block(there if sending else here, at)
        src = mine.at[pl.ds(*at)] if sending and there == (0, 0) else dst
        i = index[name]
        return remote(src, dst, ssem.at[i], rsem.at[i], link_to[link])

    def f_send(name):
        copy = f_copy(name, True)
        copy.start()
        sends.append(copy)

    started = set()

    def start_ready(have):
        for name in sorted(plan, key=lambda n: ({"Y": 0, "Z": 1, "YZ": 2, "ZY": 3}[n[0]], abs(n[1]), str(n))):
            if name not in started and all(a in have for a in plan[name][4]):
                started.add(name)
                f_send(name)

    def s_copy(kind, dz, sending):
        i = len(names) + DZ.index(dz) * 2 + (kind == "y")
        plane = core if sending else 1 - core
        at = PARTS[kind]
        ref = gath.at[plane, lax.rem(z + (NZ - dz), NZ), :, pl.ds(*at)]
        return remote(ref, ref, ssem.at[i], rsem.at[i], link_to["core"])

    need = {}
    for dz in DZ:
        zs = [] if dz == 0 else ([("Z", dz)] if dz != 4 else [("Z", 4, 1), ("Z", 4, -1)])
        need[("z", dz)] = zs + [("ZY", dz, s) for s in (1, -1, 2)]
        need[("y", dz)] = (
            [("Y", 1), ("Y", -1), ("Y", 2, 1), ("Y", 2, -1)] if dz == 0 else [("YZ", dz, s) for s in (0, 1, -1, 2)]
        )

    def share(have):
        for key in list(need):
            if all(a in have for a in need[key]):
                copy = s_copy(*key, True)
                copy.start()
                sends.append(copy)
                del need[key]

    have = set()
    start_ready(have)
    keep = pltpu.make_async_copy(mine, gath.at[core, z, y], lsem.at[0])
    keep.start()

    for i in range(rows):
        zero = jnp.where(agg_ref[i, 0] == 0, p_ref[i, 0], p_ref[i, 1])
        one = jnp.where(agg_ref[i, 0] == 0, p_ref[i, 1], p_ref[i, 0])
        ordered[i, :, :T] = zero
        ordered[i, :, T:] = one
    dacc[...] = jnp.zeros_like(dacc)
    per = ao_ref.shape[1]

    def diag_rows(lo, hi):
        def row(i, _):
            left_t[i] = ordered[i].T
            for k in range(per):
                part = jnp.dot(left_t[i], ad_ref[i, k], preferred_element_type=jnp.float32)
                dacc[...] += jnp.dot(
                    part.astype(jnp.bfloat16), ordered[dcols_ref[i, k]], preferred_element_type=jnp.float32
                ).reshape(dacc.shape)
            return 0

        lax.fori_loop(lo, hi, row, 0)

    def left_copy(slot, part):
        ref = left.at[slot, pl.ds(part * half, half)]
        return pltpu.make_async_copy(
            ref, left_out.at[slot, pl.ds(part * half, half)], lsem.at[1 + slot * 2 + part]
        )

    def left_rows(slot, part):
        def row(i, _):
            for k in range(per):
                tile = ao_ref[i, k] if slot == 0 else a_all[slot, i, k]
                left[slot, i, k] = jnp.dot(
                    left_t[i], tile, preferred_element_type=jnp.float32
                ).astype(left.dtype)
            return 0

        lax.fori_loop(part * half, part * half + half, row, 0)
        left_copy(slot, part).start()

    def d_copy(d, sending):
        quarter = dacc.shape[1] // 4
        src = dacc.at[:, pl.ds(pl.multiple_of(xat[d] * quarter, quarter), quarter)]
        return remote(src, drecv.at[d - 1], xs_sem.at[8 + d], xr_sem.at[8 + d], link_to[d])

    def send_diag():
        for d in (1, 2, 3):
            copy = d_copy(d, True)
            copy.start()
            sends.append(copy)

    def a_take(name, then=None):
        a_copy(name, False).wait_recv()
        if then:
            a_send(then)

    events = [(t, 1, name) for name, t in flood_order(plan).items()]
    steps = [
        (1.0, lambda: diag_rows(0, 2)), (3.5, lambda: diag_rows(2, 4)),
        (5.5, lambda: diag_rows(4, 6)), (7.5, lambda: diag_rows(6, 8)),
        (7.6, send_diag),
        (9.5, lambda: a_take(("r", 0), ("r", 2))), (9.6, lambda: a_take(("l", 1), ("l", 2))),
        (10.5, lambda: left_rows(0, 0)), (12.0, lambda: left_rows(0, 1)),
        (13.5, lambda: left_rows(1, 0)), (15.0, lambda: left_rows(3, 1)),
        (18.0, lambda: (a_take(("r", 1)), left_rows(1, 1))),
        (19.5, lambda: (a_take(("l", 0)), left_rows(3, 0))),
    ]
    events += [(t, 0, step) for t, step in steps]
    kept = False
    for _, kind, item in sorted(events, key=lambda e: (e[0], e[1], str(e[2]) if e[1] else "")):
        if kind == 0:
            item()
            continue
        f_copy(item, False).wait_recv()
        have.add(item)
        start_ready(have)
        if not kept:
            kept = True
            keep.wait()
        share(have)
    for name, part in ((("r", 2), 0), (("l", 2), 1)):
        a_take(name)
        left_rows(2, part)

    quarter = dacc.shape[1] // 4
    total = dacc[:, pl.ds(pl.multiple_of(x * quarter, quarter), quarter)]
    for d in (1, 2, 3):
        d_copy(d, False).wait_recv()
        total = total + drecv[d - 1]
        c_copy(d, False).wait_recv()
    own_ref[:, 0] = total[:, :, :T]
    own_ref[:, 1] = total[:, :, T:]
    cols_ref[...] = ctab[...]

    for dz in DZ:
        for kind in ("z", "y"):
            s_copy(kind, dz, False).wait_recv()
    fetch = pltpu.make_async_copy(gath.at[:, :, :, pl.ds(4 * T, 16)], ext, lsem.at[9])
    fetch.start()
    fetch.wait()
    line = me // (T // 4)
    tail = ext[...].reshape(2 * NZ * NY, 16, T).astype(jnp.float32)
    pick = lax.broadcasted_iota(jnp.int32, tail.shape, 1) == line
    tbl_ref[...] = jnp.sum(jnp.where(pick, tail, 0.0), axis=1).astype(jnp.int32)

    for copy in sends:
        copy.wait_send()
    for slot in range(4):
        for part in range(2):
            left_copy(slot, part).wait()


def gather_all(a_diag, diag_cols, a_offd, offd_cols, prolong, aggregate, send_rows):
    rows, per, _, _ = a_offd.shape
    vmem = pl.BlockSpec(memory_space=pltpu.VMEM)
    smem = pl.BlockSpec(memory_space=pltpu.SMEM)
    any_space = pl.BlockSpec(memory_space=pl.ANY)
    copies = len(flood_plan()) + 2 * len(DZ)
    bf16, f32 = jnp.bfloat16, jnp.float32
    return pl.pallas_call(
        gather_kernel,
        in_specs=[smem, smem, vmem, vmem, vmem, vmem, vmem],
        out_specs=[any_space, any_space, vmem, vmem, vmem],
        out_shape=[
            jax.ShapeDtypeStruct((2, NZ, NY, ROWS, T), bf16),
            jax.ShapeDtypeStruct((4, rows, per, 2 * T, T), bf16),
            jax.ShapeDtypeStruct((2, 2, T // 4, T), f32),
            jax.ShapeDtypeStruct((2 * NZ * NY, T), jnp.int32),
            jax.ShapeDtypeStruct((4, rows, T), jnp.int32),
        ],
        scratch_shapes=[
            pltpu.VMEM((ROWS, T), bf16),
            pltpu.VMEM((rows, T, 2 * T), bf16),
            pltpu.VMEM((rows, 2 * T, T), bf16),
            pltpu.VMEM((4, rows, per, T, T), bf16),
            pltpu.VMEM((4, rows, per, 2 * T, T), bf16),
            pltpu.VMEM((2, T, 2 * T), f32),
            pltpu.VMEM((3, 2, T // 4, 2 * T), f32),
            pltpu.VMEM((4, rows, T), jnp.int32),
            pltpu.VMEM((2, NZ, NY, 16, T), bf16),
            pltpu.SemaphoreType.DMA((copies,)),
            pltpu.SemaphoreType.DMA((copies,)),
            pltpu.SemaphoreType.DMA((12,)),
            pltpu.SemaphoreType.DMA((12,)),
            pltpu.SemaphoreType.DMA((10,)),
        ],
        compiler_params=pltpu.CompilerParams(
            collective_id=0, has_side_effects=True, vmem_limit_bytes=32 << 20
        ),
        name="gather_all",
    )(aggregate, diag_cols, offd_cols, send_rows.reshape(2, T), prolong, a_diag, a_offd)


def offd_kernel(me_ref, tbl_ref, cols_ref, l_ref, gath_ref, out_ref, rbuf, acc, sem):
    i = pl.program_id(0)
    rows = pl.num_programs(0)
    groups, _, per, _, _ = l_ref.shape
    count = groups * per
    base = lax.rem(me_ref[0], T // 4) * 4

    def place_of(g, r, k):
        col = cols_ref[g, r, k]
        node = col // 4
        slot = lax.rem(node, 2) * (NZ * NY) + node // 2
        return slot, tbl_ref[slot, base + lax.rem(col, 4)]

    @pl.when(i == 0)
    def _():
        def fetch(r, _):
            for t in range(count):
                slot, row = place_of(t // per, r, t % per)
                pair = gath_ref.at[slot, pl.ds(pl.multiple_of((row // 2) * T, T), T)]
                pltpu.make_async_copy(pair, rbuf.at[r, t], sem.at[r]).start()
            return 0

        lax.fori_loop(0, rows, fetch, 0)
        acc[...] = jnp.zeros_like(acc)

    pltpu.make_async_copy(gath_ref.at[pl.ds(0, count), pl.ds(0, T)], rbuf.at[i], sem.at[i]).wait()
    high = lax.broadcasted_iota(jnp.int32, (T, T), 1) >= H
    for t in range(count):
        slot, row = place_of(t // per, i, t % per)
        odd = lax.rem(row, 2) == 1
        y = jnp.dot(l_ref[t // per, 0, t % per], rbuf[i, t], preferred_element_type=jnp.float32)
        kept = jnp.where(odd, y[T:], y[:T])
        moved = jnp.where(odd, y[:T], y[T:])
        acc[slot] += jnp.where(high == odd, kept, pltpu.roll(moved, H, 1))

    @pl.when(i == rows - 1)
    def _():
        quarter = out_ref.shape[2]
        for g in range(out_ref.shape[0]):
            out_ref[g] = acc[:, g * quarter : (g + 1) * quarter, :].astype(out_ref.dtype)


def offd_terms(me, table, cols, left, gathered):
    groups, rows, per, _, _ = left.shape
    count = groups * per
    nodes = gathered.shape[0]
    quarter = T // groups
    return pl.pallas_call(
        offd_kernel,
        grid_spec=pltpu.PrefetchScalarGridSpec(
            num_scalar_prefetch=3,
            grid=(rows,),
            in_specs=[
                pl.BlockSpec((groups, 1, per, 2 * T, T), lambda i, *_: (0, i, 0, 0, 0)),
                pl.BlockSpec(memory_space=pl.ANY),
            ],
            out_specs=pl.BlockSpec((groups, nodes, quarter, T), lambda i, *_: (0, 0, 0, 0)),
            scratch_shapes=[
                pltpu.VMEM((rows, count, T, T), jnp.bfloat16),
                pltpu.VMEM((nodes, T, T), jnp.float32),
                pltpu.SemaphoreType.DMA((rows,)),
            ],
        ),
        out_shape=jax.ShapeDtypeStruct((groups, nodes, quarter, T), jnp.bfloat16),
        compiler_params=pltpu.CompilerParams(vmem_limit_bytes=40 << 20),
        cost_estimate=pl.CostEstimate(
            flops=rows * count * 4 * T**3, bytes_accessed=rows * count * 6 * T * T, transcendentals=0
        ),
        name="offd_terms",
    )(me, table, cols, left, gathered)


def place_kernel(map_ref, me_ref, x_ref, d_ref, out_ref):
    slots = out_ref.shape[1]
    quarter = out_ref.shape[2]
    high = lax.broadcasted_iota(jnp.int32, (quarter, T), 1) >= H
    me = me_ref[0]

    def place(m, _):
        gid = map_ref[m]
        node, agg = gid // CR1, gid % CR1
        own = node == me
        slot = lax.rem(node, 2) * (NZ * NY) + node // 2
        left = x_ref[2 * agg, slot].astype(jnp.float32)
        right = x_ref[2 * agg + 1, slot].astype(jnp.float32)
        top = jnp.where(high, pltpu.roll(right, H, 1), left)
        low = jnp.where(high, right, pltpu.roll(left, H, 1))
        out_ref[0, m] = jnp.where(own, d_ref[0, agg], top).astype(out_ref.dtype)
        out_ref[1, m] = jnp.where(own, d_ref[1, agg], low).astype(out_ref.dtype)
        return 0

    lax.fori_loop(0, slots, place, 0, unroll=2)


def place_slots(col_map, me, arrived, own):
    slots = col_map.shape[0]
    quarter = arrived.shape[2]
    vmem = pl.BlockSpec(memory_space=pltpu.VMEM)
    smem = pl.BlockSpec(memory_space=pltpu.SMEM)
    return pl.pallas_call(
        place_kernel,
        in_specs=[smem, smem, vmem, vmem],
        out_specs=vmem,
        out_shape=jax.ShapeDtypeStruct((CR1, slots, quarter, T), jnp.bfloat16),
        compiler_params=pltpu.CompilerParams(vmem_limit_bytes=16 << 20),
        name="place_slots",
    )(col_map, me, arrived, own)


def per_device(
    a_diag, diag_cols, a_offd, offd_cols, prolong, aggregate, send_rows, ghost_agg, coarse_map
):
    me = lax.axis_index("rows").reshape(1)
    gathered, left, own, table, cols = gather_all(
        a_diag, diag_cols, a_offd, offd_cols, prolong, aggregate, send_rows
    )
    gathered = gathered.reshape(2 * NZ * NY, ROWS, T)
    offd = offd_terms(me, table, cols, left, gathered)
    arrived = lax.all_to_all(offd, "grp", split_axis=0, concat_axis=0, tiled=True)
    return place_slots(coarse_map[0], me, arrived, own)


def solution(mesh):
    in_specs = (
        P("rows", "grp", None, None),
        P("rows", "grp"),
        P("rows", "grp", None, None),
        P("rows", "grp"),
        P("rows", None, None, None),
        P("rows", None),
        P("rows", None, None),
        P("rows", None, None, None),
        P("rows", None),
    )
    out_specs = P("rows", None, "grp", None)
    return jax.shard_map(
        per_device, mesh=mesh, in_specs=in_specs, out_specs=out_specs, check_vma=False
    )
```

time: 201 us -> 99.1 us (0.49)
  waiting for transfers between devices: 80.6 us -> 0 us
  blocking collectives: 62.8 us -> 29.4 us
  Pallas kernels: 28.6 us -> 59.6 us
  between operations: 13.2 us -> 0.05 us
  starting transfers between devices: 4.02 us -> 0 us
  other arithmetic: 3.79 us -> 0 us
  local copies, waits for them, and re-layouts: 7.66 us -> 9.76 us
    all_gather x2 -> x0, blocking collectives: 62.8 us -> none  [the longest x1 54.3 us: per_device(): rows_all = lax.all_gather(send_rows, 'rows', axis=0, tiled=True)]
    all_gather x2 -> x0, waiting for transfers between devices: 58 us -> none  [the longest x1 58 us: per_device(): gathered = lax.all_gather(mine, 'rows', axis=0, tiled=True)]
    pallas_call x2 -> x1, Pallas kernels: 14.9 us -> 45.1 us  [gather_all(): pl.pallas_call(gather_kernel, in_specs=[smem, smem, vmem, vmem, vmem, vme...]
    all_to_all x0 -> x1, blocking collectives: none -> 29.4 us  [per_device(): lax.all_to_all(offd, 'grp', split_axis=0, concat_axis=0, tiled=True)]
    reduce_scatter x1 -> x0, waiting for transfers between devices: 21.9 us -> none  [per_device(): own = lax.psum_scatter(partial, 'grp', scatter_dimension=2, tiled=True)]
    unnamed x15 -> x14, local copies, waits for them, and re-layouts: 4.41 us -> 9.66 us
    all_to_all x1 -> x0, starting transfers between devices: 3.98 us -> none  [per_device(): lax.all_to_all(offd, 'grp', split_axis=0, concat_axis=0, tiled=True)]
  transfers between devices with their start and end apart: 4 -> 0, of which waited for: 2 -> 0; matrix products, arithmetic and copies ran while one was open for 4% -> 0% of each run, Pallas kernels for 7% -> 0%
where the time goes in v2:
time: 99.1 us; the launch traced here: 98.8 us
  Pallas kernels  59.6 us (60%)
  blocking collectives  29.4 us (30%)
  local copies, waits for them, and re-layouts  9.76 us (10%)
    pallas_call x1, Pallas kernels, gather_all(): pl.pallas_call(gather_kernel, in_specs=[smem, smem, vmem, vmem, vmem, vme...  45.1 us
    all_to_all x1, blocking collectives, per_device(): lax.all_to_all(offd, 'grp', split_axis=0, concat_axis=0, tiled=True)  29.4 us
    unnamed x14, local copies, waits for them, and re-layouts  9.66 us
    pallas_call x1, Pallas kernels, offd_terms(): pl.pallas_call(offd_kernel, grid_spec=pltpu.PrefetchScalarGridSpec(num_sc...  8.09 us
    pallas_call x1, Pallas kernels, place_slots(): pl.pallas_call(place_kernel, in_specs=[smem, smem, vmem, vmem], out_specs...  6.42 us

profile of v2, /device:TPU:1, one launch (start us, length us, event | category | flops | bytes accessed | tf_op | source)
XLA Modules:
  0.0 98.8 jit_solution(3036250735483856452)
XLA Ops:
  0.0 0.8 copy.15.dcols_ref
  0.8 0.8 copy.16.ocols_ref
  1.5 0.8 copy.14.agg_ref
  2.3 0.8 copy.13
  3.0 0.1 reshape.10.srows_ref
  3.1 0.0 copy-start.1
  3.2 1.1 %copy-done.1 = bf16[8,3,128,128]{3,2,1,0:T(8,128)(2,1)S(1)} copy-done((bf16[8,3,128,128]{3,2,1,0:T(8,128)(2,1)S(1)}, bf16[8,3,128,128]{3,2,1,0:T(8,128)(2,1)}, u32[]{:S(2)}) %copy-start.1) | copy-done | bytes 786456
  4.3 0.0 copy-start.2
  4.3 1.1 %copy-done.2 = bf16[8,3,128,128]{3,2,1,0:T(8,128)(2,1)S(1)} copy-done((bf16[8,3,128,128]{3,2,1,0:T(8,128)(2,1)S(1)}, bf16[8,3,128,128]{3,2,1,0:T(8,128)(2,1)}, u32[]{:S(2)}) %copy-start.2) | copy-done | bytes 786456
  5.4 0.0 copy-start.3
  5.4 1.0 %copy-done.3 = bf16[8,2,128,128]{3,2,1,0:T(8,128)(2,1)S(1)} copy-done((bf16[8,2,128,128]{3,2,1,0:T(8,128)(2,1)S(1)}, bf16[8,2,128,128]{3,2,1,0:T(8,128)(2,1)}, u32[]{:S(2)}) %copy-start.3) | copy-done | bytes 524312
  6.5 45.1 %gather_all.1 = (bf16[2,8,4,528,128]{4,3,2,1,0:T(8,128)(2,1)S(1)}, bf16[4,8,3,256,128]{4,3,2,1,0:T(8,128)(2,1)S(1)}, f32[2,2,32,128]{3,2,1,0:T(8,128)S(1)}, s32[64,128]{1,0:T(8,128)S(1)}, s32[4,8,128]{2,1,0:T(8,128)S(1)}) custom-call(s32[8,2]{1,0:T(8,128)S(1)} %copy.14.agg_ref, s32[8,3]{1,0:T(8,128)S(1)} %copy.15.dcols_ref, s32[8,3]{1,0:T(8,128)S(1)} %copy.16.ocols_ref, ...), custom_call_target="tpu_custom_call" | custom-call | tf_op jit(solution)/shard_map/gather_all/pallas_call | solution.py:351
  51.6 0.0 copy-start
  51.6 3.3 %copy-done = bf16[2,8,4,528,128]{4,3,2,1,0:T(8,128)(2,1)} copy-done((bf16[2,8,4,528,128]{4,3,2,1,0:T(8,128)(2,1)}, bf16[2,8,4,528,128]{4,3,2,1,0:T(8,128)(2,1)S(1)}, u32[]{:S(2)}) %copy-start) | copy-done | bytes 8650776
  54.9 8.1 %offd_terms.1 = bf16[4,64,32,128]{3,2,1,0:T(8,128)(2,1)S(1)} custom-call(s32[1]{0:T(128)} %bitcast.1.me_ref, s32[64,128]{1,0:T(8,128)S(1)} %get-tuple-element.10.tbl_ref, s32[4,8,128]{2,1,0:T(8,128)S(1)} %get-tuple-element.11.cols_ref, bf16[4,8,3,256,128]{4,3,2,1,0:T(8,128)(2,1)S(1)} %get-tuple-element.12.l_ref, bf16[64,528,128]{2,1,0:T(8,128)(2,1)} %bitcast.3), custom_call_target="tpu_custom_call" | custom-call | flops 805306368 | bytes 9437184 | tf_op jit(solution)/shard_map/offd_terms/pallas_call | solution.py:432
  63.0 0.0 copy-start.4
  63.0 29.4 %all_to_all.5.x_ref = bf16[4,64,32,128]{3,2,1,0:T(8,128)(2,1)S(1)} all-to-all(bf16[4,64,32,128]{3,2,1,0:T(8,128)(2,1)S(1)} %offd_terms.1), channel_id=1, replica_groups=mesh['rows'=64,'grp'=4] {'grp'}, dimensions={0} | all-to-all | bytes 4194304 | tf_op jit(solution)/shard_map/all_to_all | solution.py:503
  92.4 0.0 copy-done.4
  92.4 6.4 %place_slots.1 = bf16[2,98,32,128]{3,2,1,0:T(8,128)(2,1)} custom-call(s32[98]{0:T(128)S(1)} %bitcast.4, s32[1]{0:T(128)} %bitcast.1.me_ref, bf16[4,64,32,128]{3,2,1,0:T(8,128)(2,1)S(1)} %all_to_all.5.x_ref, f32[2,2,32,128]{3,2,1,0:T(8,128)S(1)} %get-tuple-element.14.d_ref), custom_call_target="tpu_custom_call" | custom-call | tf_op jit(solution)/shard_map/place_slots/pallas_call | solution.py:484
Async XLA Ops:
  3.1 1.1 %copy-start.1 = (bf16[8,3,128,128]{3,2,1,0:T(8,128)(2,1)S(1)}, bf16[8,3,128,128]{3,2,1,0:T(8,128)(2,1)}, u32[]{:S(2)}) copy-start(bf16[8,3,128,128]{3,2,1,0:T(8,128)(2,1)} %ad_ref.1) | copy-start | bytes 2359300
  4.3 1.1 %copy-start.2 = (bf16[8,3,128,128]{3,2,1,0:T(8,128)(2,1)S(1)}, bf16[8,3,128,128]{3,2,1,0:T(8,128)(2,1)}, u32[]{:S(2)}) copy-start(bf16[8,3,128,128]{3,2,1,0:T(8,128)(2,1)} %ao_ref.1) | copy-start | bytes 2359300
  5.4 1.0 %copy-start.3 = (bf16[8,2,128,128]{3,2,1,0:T(8,128)(2,1)S(1)}, bf16[8,2,128,128]{3,2,1,0:T(8,128)(2,1)}, u32[]{:S(2)}) copy-start(bf16[8,2,128,128]{3,2,1,0:T(8,128)(2,1)} %p_ref.1) | copy-start | bytes 1572868
  51.6 3.3 %copy-start = (bf16[2,8,4,528,128]{4,3,2,1,0:T(8,128)(2,1)}, bf16[2,8,4,528,128]{4,3,2,1,0:T(8,128)(2,1)S(1)}, u32[]{:S(2)}) copy-start(bf16[2,8,4,528,128]{4,3,2,1,0:T(8,128)(2,1)S(1)} %get-tuple-element.13) | copy-start | bytes 25952260
  63.0 29.4 %copy-start.4 = (s32[1,98]{1,0:T(1,128)S(1)}, s32[1,98]{1,0:T(1,128)}, u32[]{:S(2)}) copy-start(s32[1,98]{1,0:T(1,128)} %param.16) | copy-start | bytes 1180

commit v3 on v2

v3 whole, which is shorter than its diff:
```python
import functools

import jax
import jax.numpy as jnp
from jax import lax
from jax.experimental import pallas as pl
from jax.experimental.pallas import tpu as pltpu
from jax.sharding import PartitionSpec as P

CR1 = 2
T = 128
H = T // 2


ROWS = 528
ZR = 320
NZ, NY = 8, 4
MESH = pl.DeviceIdType.MESH
PARTS = {"z": (0, ZR), "za": (0, ZR // 2), "zb": (ZR // 2, ZR // 2),
         "y": (ZR, ROWS - ZR), "ya": (ZR, 112), "yb": (ZR + 112, ROWS - ZR - 112)}
DZ = (0, 1, -1, 2, -2, 3, -3, 4)
LATE_UP = (0, 1, 2, 3)


def flood_plan():
    plan = {}

    def add(name, link, there, here, part, after):
        plan[name] = (link, there, here, part, tuple(after))

    for sign, link in ((1, "z+"), (-1, "z-")):
        for d in range(1, 5):
            part = "z" if d < 4 else ("za" if sign == 1 else "zb")
            after = [] if d == 1 else [("Z", sign * (d - 1))]
            here = sign * d if d < 4 else 4
            name = ("Z", here) if d < 4 else ("Z", 4, sign)
            add(name, link, (sign * (d - 1), 0), (here, 0), part, after)
    for e in DZ:
        have = [] if e == 0 else ([("Z", e)] if e != 4 else [("Z", 4, 1), ("Z", 4, -1)])
        for sign, link in ((1, "y+"), (-1, "y-")):
            add(("ZY", e, sign), link, (e, 0), (e, sign), "z", have)
        sign = 1 if e in LATE_UP else -1
        add(("ZY", e, 2), "y+" if sign == 1 else "y-", (e, sign), (e, 2), "z", [("ZY", e, sign)])
    for sign, link in ((1, "y+"), (-1, "y-")):
        add(("Y", sign), link, (0, 0), (0, sign), "y", [])
        add(("Y", 2, sign), link, (0, sign), (0, 2), "ya" if sign == 1 else "yb", [("Y", sign)])
    for sign, link in ((1, "z+"), (-1, "z-")):
        for d in range(1, 5):
            for dy in (0, 1, -1, 2):
                if d == 4 and (dy in (0, 1)) != (sign == 1):
                    continue
                if d > 1:
                    after = [("YZ", sign * (d - 1), dy)]
                elif dy == 0:
                    after = []
                else:
                    after = [("Y", dy)] if dy != 2 else [("Y", 2, 1), ("Y", 2, -1)]
                here = sign * d if d < 4 else 4
                add(("YZ", here, dy), link, (sign * (d - 1), dy), (here, dy), "y", after)
    return plan


def flood_order(plan):
    free = {}
    arrive, waiting = {}, dict(plan)
    rank = {"Y": 0, "Z": 1, "YZ": 2, "ZY": 3}
    while len(arrive) < len(plan):
        best = None
        for name, (link, _, _, part, after) in waiting.items():
            if any(a not in arrive for a in after):
                continue
            start = max([arrive[a] for a in after] + [free.get(link, 0.0)])
            key = (start, rank[name[0]], abs(name[1]), str(name))
            if best is None or key < best[0]:
                best = (key, name, start, link, part)
        _, name, start, link, part = best
        end = start + PARTS[part][1] * 256 / 50e3
        free[link] = end
        arrive[name] = end + 1.5
        del waiting[name]
    return arrive


def gather_kernel(
    agg_ref, dcols_ref, ocols_ref, srows_ref, p_hbm, ad_hbm, ao_hbm,
    gath, left, own_ref, tbl_ref, cols_ref,
    p_ref, ad_ref, mine, stage, tiles, ordered, left_t, a_all, dacc, dsend, drecv, ctab,
    ssem, rsem, xs_sem, xr_sem, lsem,
):
    me = lax.axis_index("rows")
    x = lax.axis_index("grp")
    core = lax.rem(me, 2)
    y = lax.rem(me // 2, NY)
    z = me // (2 * NY)

    def row_of(zz, yy, cc):
        return (zz * NY + yy) * 2 + cc

    up_z, dn_z = lax.rem(z + 1, NZ), lax.rem(z + NZ - 1, NZ)
    up_y, dn_y = lax.rem(y + 1, NY), lax.rem(y + NY - 1, NY)
    xat = [lax.rem(x + d, 4) for d in range(4)]
    link_to = {
        "z+": (row_of(up_z, y, core), x),
        "z-": (row_of(dn_z, y, core), x),
        "y+": (row_of(z, up_y, core), x),
        "y-": (row_of(z, dn_y, core), x),
        "core": (row_of(z, y, 1 - core), x),
        1: (me, xat[1]),
        2: (me, xat[2]),
        3: (me, xat[3]),
    }
    barrier = pltpu.get_barrier_semaphore()
    for device in link_to.values():
        pl.semaphore_signal(barrier, inc=1, device_id=device, device_id_type=MESH)

    loads = [
        pltpu.make_async_copy(p_hbm, p_ref, lsem.at[1]),
        pltpu.make_async_copy(ao_hbm, a_all.at[0], lsem.at[2]),
        pltpu.make_async_copy(ad_hbm, ad_ref, lsem.at[3]),
    ]
    for load in loads:
        load.start()

    sends = []

    def remote(src, dst, s, r, device):
        return pltpu.make_async_remote_copy(
            src_ref=src, dst_ref=dst, send_sem=s, recv_sem=r, device_id=device, device_id_type=MESH
        )

    half = ao_hbm.shape[0] // 2
    first, second = pl.ds(0, half), pl.ds(half, half)
    a_plan = {
        ("r", 0): (0, 1, first, 1), ("r", 1): (0, 1, second, 1), ("r", 2): (1, 2, first, 1),
        ("l", 1): (0, 3, second, 3), ("l", 0): (0, 3, first, 3), ("l", 2): (3, 2, second, 3),
    }
    a_index = {name: i for i, name in enumerate(a_plan)}

    def a_copy(name, sending):
        src_slot, dst_slot, part, to = a_plan[name]
        dst = a_all.at[dst_slot, part]
        src = (ao_hbm if src_slot == 0 else a_all.at[src_slot]).at[part] if sending else dst
        i = a_index[name]
        return remote(src, dst, xs_sem.at[i], xr_sem.at[i], link_to[to])

    def a_send(name):
        copy = a_copy(name, True)
        copy.start()
        sends.append(copy)

    def c_copy(d):
        return remote(ctab.at[0], ctab.at[d], xs_sem.at[5 + d], xr_sem.at[5 + d], link_to[d])

    lane = lax.broadcasted_iota(jnp.int32, (T, T), 1)
    rows = p_hbm.shape[0]
    stage[...] = jnp.zeros_like(stage)
    stage[0 : srows_ref.shape[0], 0 : srows_ref.shape[1]] = srows_ref[...].astype(jnp.float32)
    ctab[0, 0 : ocols_ref.shape[0], 0 : ocols_ref.shape[1]] = ocols_ref[...]
    loads[0].wait()

    def tile(i, a):
        flip = agg_ref[0, i] == a
        return jnp.where(flip, p_ref[i, 0], p_ref[i, 1]).astype(jnp.float32)

    for p in range(rows // 2):
        pair = None
        for r in range(2):
            for a in range(2):
                at = r * 64 + a * 32
                moved = pltpu.roll(tile(2 * p + r, a), lax.rem(at + T - 32 * x, T), 1)
                pair = moved if pair is None else jnp.where(lane >= at, moved, pair)
        mine[p * T : (p + 1) * T, :] = pair.astype(mine.dtype)
    mine[4 * T :, :] = stage[...].astype(mine.dtype)

    plan = flood_plan()
    names = sorted(plan, key=str)
    index = {name: i for i, name in enumerate(names)}

    def block(offset, rows_at):
        dz, dy = offset
        return gath.at[core, lax.rem(z + (NZ - dz), NZ), lax.rem(y + (NY - dy), NY), pl.ds(*rows_at)]

    def f_copy(name, sending):
        link, there, here, part, _ = plan[name]
        at = PARTS[part]
        dst = block(there if sending else here, at)
        src = mine.at[pl.ds(*at)] if sending and there == (0, 0) else dst
        i = index[name]
        return remote(src, dst, ssem.at[i], rsem.at[i], link_to[link])

    started = set()

    def start_ready(have):
        order = {"Y": 0, "Z": 1, "YZ": 2, "ZY": 3}
        for name in sorted(plan, key=lambda n: (order[n[0]], abs(n[1]), str(n))):
            if name not in started and all(a in have for a in plan[name][4]):
                started.add(name)
                copy = f_copy(name, True)
                copy.start()
                sends.append(copy)

    def s_copy(kind, dz, sending):
        i = len(names) + DZ.index(dz) * 2 + (kind == "y")
        plane = core if sending else 1 - core
        ref = gath.at[plane, lax.rem(z + (NZ - dz), NZ), :, pl.ds(*PARTS[kind])]
        return remote(ref, ref, ssem.at[i], rsem.at[i], link_to["core"])

    need = {}
    for dz in DZ:
        zs = [] if dz == 0 else ([("Z", dz)] if dz != 4 else [("Z", 4, 1), ("Z", 4, -1)])
        need[("z", dz)] = zs + [("ZY", dz, s) for s in (1, -1, 2)]
        need[("y", dz)] = (
            [("Y", 1), ("Y", -1), ("Y", 2, 1), ("Y", 2, -1)]
            if dz == 0
            else [("YZ", dz, s) for s in (0, 1, -1, 2)]
        )

    def share(have):
        for key in list(need):
            if all(a in have for a in need[key]):
                copy = s_copy(*key, True)
                copy.start()
                sends.append(copy)
                del need[key]

    pl.semaphore_wait(barrier, len(link_to))
    have = set()
    start_ready(have)
    for name in (("r", 0), ("l", 1), ("r", 1), ("l", 0)):
        a_send(name)
    for d in (1, 2, 3):
        copy = c_copy(d)
        copy.start()
        sends.append(copy)
    keep = pltpu.make_async_copy(mine, gath.at[core, z, y], lsem.at[0])
    keep.start()

    per = ao_hbm.shape[1]

    def order_rows(lo, hi):
        def row(i, _):
            zero, one = tile(i, 0), tile(i, 1)
            tiles[0] = zero.astype(tiles.dtype)
            tiles[1] = one.astype(tiles.dtype)
            left_t[i, :T] = tiles[0].T
            left_t[i, T:] = tiles[1].T
            z32, z64, z96 = (pltpu.roll(zero, s, 1) for s in (32, 64, 96))
            o32, o64, o96 = (pltpu.roll(one, s, 1) for s in (32, 64, 96))
            low = jnp.where(lane < 32, zero, jnp.where(lane < 64, o32, jnp.where(lane < 96, z32, o64)))
            top = jnp.where(lane < 32, z64, jnp.where(lane < 64, o96, jnp.where(lane < 96, z96, one)))
            ordered[i, :, :T] = low.astype(ordered.dtype)
            ordered[i, :, T:] = top.astype(ordered.dtype)
            return 0

        lax.fori_loop(lo, hi, row, 0)

    def diag_rows(lo, hi):
        def row(i, _):
            for k in range(per):
                part = jnp.dot(left_t[i], ad_ref[i, k], preferred_element_type=jnp.float32)
                dacc[...] += jnp.dot(
                    part.astype(jnp.bfloat16), ordered[dcols_ref[k, i]], preferred_element_type=jnp.float32
                )
            return 0

        lax.fori_loop(lo, hi, row, 0)

    def left_rows(slot, part):
        def row(i, _):
            for k in range(per):
                left[slot, i, k] = jnp.dot(
                    left_t[i], a_all[slot, i, k], preferred_element_type=jnp.float32
                ).astype(left.dtype)
            return 0

        lax.fori_loop(part * half, part * half + half, row, 0)

    def d_copy(d):
        return remote(
            dsend.at[xat[d]], drecv.at[d - 1], xs_sem.at[8 + d], xr_sem.at[8 + d], link_to[d]
        )

    def send_diag():
        for q in range(4):
            at = slice((q // 2) * T, (q // 2 + 1) * T)
            zero, one = dacc[:T, at], dacc[T:, at]
            if q % 2 == 0:
                one = pltpu.roll(one, H, 1)
            else:
                zero = pltpu.roll(zero, H, 1)
            dsend[q] = jnp.where(lane < H, zero, one)
        for d in (1, 2, 3):
            copy = d_copy(d)
            copy.start()
            sends.append(copy)

    def a_take(name, then=None):
        a_copy(name, False).wait_recv()
        if then:
            a_send(then)

    def begin():
        dacc[...] = jnp.zeros_like(dacc)
        loads[1].wait()
        loads[2].wait()
        order_rows(0, rows)

    events = [(t, 1, name) for name, t in flood_order(plan).items()]
    steps = [
        (0.0, begin), (1.5, lambda: diag_rows(0, 2)), (3.5, lambda: diag_rows(2, 4)),
        (5.5, lambda: diag_rows(4, 6)), (7.5, lambda: diag_rows(6, 8)),
        (7.6, send_diag),
        (9.5, lambda: a_take(("r", 0), ("r", 2))), (9.6, lambda: a_take(("l", 1), ("l", 2))),
        (10.5, lambda: left_rows(0, 0)), (12.0, lambda: left_rows(0, 1)),
        (13.5, lambda: left_rows(1, 0)), (15.0, lambda: left_rows(3, 1)),
        (18.0, lambda: (a_take(("r", 1)), left_rows(1, 1))),
        (19.5, lambda: (a_take(("l", 0)), left_rows(3, 0))),
    ]
    events += [(t, 0, step) for t, step in steps]
    kept = False
    for _, kind, item in sorted(events, key=lambda e: (e[0], e[1], str(e[2]) if e[1] else "")):
        if kind == 0:
            item()
            continue
        f_copy(item, False).wait_recv()
        have.add(item)
        start_ready(have)
        if not kept:
            kept = True
            keep.wait()
        share(have)
    for name, part in ((("r", 2), 0), (("l", 2), 1)):
        a_take(name)
        left_rows(2, part)

    total = dsend[x]
    for d in (1, 2, 3):
        d_copy(d).wait_recv()
        total = total + drecv[d - 1]
        c_copy(d).wait_recv()
    own_ref[...] = total
    cols_ref[...] = ctab[...]

    for dz in DZ:
        for kind in ("z", "y"):
            s_copy(kind, dz, False).wait_recv()
    tail = gath[:, :, :, 4 * T :, :].reshape(2 * NZ * NY * 16, T)
    pick = (lax.broadcasted_iota(jnp.int32, (T, T), 0) == me).astype(jnp.bfloat16)
    spread = jnp.dot(tail, pick, preferred_element_type=jnp.float32).reshape(2 * NZ * NY, 16, T)
    line = lax.broadcasted_iota(jnp.int32, spread.shape, 1) == lax.broadcasted_iota(
        jnp.int32, spread.shape, 2
    )
    tbl_ref[...] = jnp.sum(jnp.where(line, spread, 0.0), axis=1).astype(jnp.int32)

    for copy in sends:
        copy.wait_send()


def gather_all(a_diag, diag_cols, a_offd, offd_cols, prolong, aggregate, send_rows):
    rows, per, _, _ = a_offd.shape
    vmem = pl.BlockSpec(memory_space=pltpu.VMEM)
    smem = pl.BlockSpec(memory_space=pltpu.SMEM)
    hbm = pl.BlockSpec(memory_space=pltpu.HBM)
    copies = len(flood_plan()) + 2 * len(DZ)
    bf16, f32 = jnp.bfloat16, jnp.float32
    return pl.pallas_call(
        gather_kernel,
        in_specs=[smem, smem, vmem, vmem, hbm, hbm, hbm],
        out_specs=[vmem, vmem, vmem, vmem, vmem],
        out_shape=[
            jax.ShapeDtypeStruct((2, NZ, NY, ROWS, T), bf16),
            jax.ShapeDtypeStruct((4, rows, per, 2 * T, T), bf16),
            jax.ShapeDtypeStruct((T, T), f32),
            jax.ShapeDtypeStruct((2 * NZ * NY, T), jnp.int32),
            jax.ShapeDtypeStruct((4, 8, T), jnp.int32),
        ],
        scratch_shapes=[
            pltpu.VMEM((rows, 2, T, T), bf16),
            pltpu.VMEM((rows, per, T, T), bf16),
            pltpu.VMEM((ROWS, T), bf16),
            pltpu.VMEM((16, T), f32),
            pltpu.VMEM((2, T, T), bf16),
            pltpu.VMEM((rows, T, 2 * T), bf16),
            pltpu.VMEM((rows, 2 * T, T), bf16),
            pltpu.VMEM((4, rows, per, T, T), bf16),
            pltpu.VMEM((2 * T, 2 * T), f32),
            pltpu.VMEM((4, T, T), f32),
            pltpu.VMEM((3, T, T), f32),
            pltpu.VMEM((4, 8, T), jnp.int32),
            pltpu.SemaphoreType.DMA((copies,)),
            pltpu.SemaphoreType.DMA((copies,)),
            pltpu.SemaphoreType.DMA((12,)),
            pltpu.SemaphoreType.DMA((12,)),
            pltpu.SemaphoreType.DMA((4,)),
        ],
        compiler_params=pltpu.CompilerParams(
            collective_id=0, has_side_effects=True, vmem_limit_bytes=32 << 20
        ),
        name="gather_all",
    )(aggregate.T, diag_cols.T, offd_cols.T, send_rows[0].T, prolong, a_diag, a_offd)


def offd_kernel(me_ref, map_ref, tbl_ref, cols_ref, l_ref, gath_ref, d_ref, out_ref, acc):
    groups, rows, per, _, _ = l_ref.shape
    high = lax.broadcasted_iota(jnp.int32, (T, T), 1) >= H
    acc[...] = jnp.zeros_like(acc)

    def slot_of(node):
        return lax.rem(node, 2) * (NZ * NY) + node // 2

    def row(i, _):
        for t in range(groups * per):
            g, k = t // per, t % per
            col = cols_ref[g, k, i]
            slot = slot_of(col // 4)
            sent = tbl_ref[slot, lax.rem(col, 4)]
            odd = lax.rem(sent, 2) == 1
            right = gath_ref[slot, pl.ds(pl.multiple_of((sent // 2) * T, T), T), :]
            y = jnp.dot(l_ref[g, i, k], right, preferred_element_type=jnp.float32)
            kept = jnp.where(odd, y[T:], y[:T])
            moved = jnp.where(odd, y[:T], y[T:])
            acc[slot] += jnp.where(high == odd, kept, pltpu.roll(moved, H, 1))
        return 0

    lax.fori_loop(0, rows, row, 0)
    acc[slot_of(me_ref[0])] = d_ref[...]

    lane = lax.broadcasted_iota(jnp.int32, (T, T), 1)
    even = lax.rem(lane // 32, 2) == 0

    def pack(p, _):
        def part(j):
            gid = map_ref[2 * p + j]
            shift = lax.rem((j - lax.rem(gid, CR1)) * 32 + T, T)
            return pltpu.roll(acc[slot_of(gid // CR1)], shift, 1)

        both = jnp.where(even, part(0), part(1)).astype(out_ref.dtype)
        quarter = out_ref.shape[2]
        for g in range(out_ref.shape[0]):
            out_ref[g, p] = both[g * quarter : (g + 1) * quarter]
        return 0

    lax.fori_loop(0, out_ref.shape[1], pack, 0)


def offd_terms(me, col_map, table, cols, left, gathered, own):
    groups, rows, per, _, _ = left.shape
    nodes = gathered.shape[0]
    vmem = pl.BlockSpec(memory_space=pltpu.VMEM)
    smem = pl.BlockSpec(memory_space=pltpu.SMEM)
    return pl.pallas_call(
        offd_kernel,
        in_specs=[smem, smem, smem, smem, vmem, vmem, vmem],
        out_specs=vmem,
        out_shape=jax.ShapeDtypeStruct((groups, col_map.shape[0] // 2, T // groups, T), jnp.bfloat16),
        scratch_shapes=[pltpu.VMEM((nodes, T, T), jnp.float32)],
        compiler_params=pltpu.CompilerParams(vmem_limit_bytes=32 << 20),
        name="offd_terms",
    )(me, col_map, table, cols, left, gathered, own)


def swap_kernel(src, out, hold, ssem, rsem, lsem):
    me = lax.axis_index("rows")
    x = lax.axis_index("grp")
    at = [lax.rem(x + d, 4) for d in range(4)]
    up, down = (me, at[1]), (me, at[3])
    barrier = pltpu.get_barrier_semaphore()
    for device in (up, down):
        pl.semaphore_signal(barrier, inc=1, device_id=device, device_id_type=MESH)
    pl.semaphore_wait(barrier, 2)
    pairs = src.shape[1]
    cut = pairs // 2
    low, top = pl.ds(0, cut), pl.ds(cut, pairs - cut)

    def remote(a, b, i, device):
        return pltpu.make_async_remote_copy(
            src_ref=a, dst_ref=b, send_sem=ssem.at[i], recv_sem=rsem.at[i],
            device_id=device, device_id_type=MESH,
        )

    far = src.at[at[2]]
    sends = [
        remote(far.at[low], hold.at[low], 0, up),
        remote(far.at[top], hold.at[top], 1, down),
        remote(src.at[at[1]], out.at[x], 2, up),
        remote(src.at[at[3]], out.at[x], 3, down),
    ]
    for copy in sends:
        copy.start()
    stay = pltpu.make_async_copy(src.at[x], out.at[x], lsem)
    stay.start()
    remote(hold.at[low], hold.at[low], 0, up).wait_recv()
    sends.append(remote(hold.at[low], out.at[at[3], low], 4, up))
    sends[-1].start()
    remote(hold.at[top], hold.at[top], 1, down).wait_recv()
    sends.append(remote(hold.at[top], out.at[at[1], top], 5, down))
    sends[-1].start()
    remote(out.at[at[3]], out.at[at[3]], 2, up).wait_recv()
    remote(out.at[at[1]], out.at[at[1]], 3, down).wait_recv()
    remote(out.at[at[2], low], out.at[at[2], low], 4, up).wait_recv()
    remote(out.at[at[2], top], out.at[at[2], top], 5, down).wait_recv()
    stay.wait()
    for copy in sends:
        copy.wait_send()


def swap_slices(src):
    vmem = pl.BlockSpec(memory_space=pltpu.VMEM)
    return pl.pallas_call(
        swap_kernel,
        in_specs=[vmem],
        out_specs=vmem,
        out_shape=jax.ShapeDtypeStruct(src.shape, src.dtype),
        scratch_shapes=[
            pltpu.VMEM(src.shape[1:], src.dtype),
            pltpu.SemaphoreType.DMA((6,)),
            pltpu.SemaphoreType.DMA((6,)),
            pltpu.SemaphoreType.DMA,
        ],
        compiler_params=pltpu.CompilerParams(
            collective_id=1, has_side_effects=True, vmem_limit_bytes=16 << 20
        ),
        name="swap_slices",
    )(src)


def place_kernel(x_ref, out_ref):
    pairs, quarter = x_ref.shape[1], x_ref.shape[2]
    lane = lax.broadcasted_iota(jnp.int32, (quarter, T), 1)
    odd32 = lax.rem(lane // 32, 2) == 1
    odd64 = lane >= H

    def swap(a, b, shift, odd):
        return (
            jnp.where(odd, pltpu.roll(b, shift, 1), a),
            jnp.where(odd, b, pltpu.roll(a, T - shift, 1)),
        )

    for p in range(pairs):
        w = [x_ref[s, p].astype(jnp.float32) for s in range(4)]
        a0, a1 = swap(w[0], w[1], 32, odd32)
        b0, b1 = swap(w[2], w[3], 32, odd32)
        c00, c10 = swap(a0, b0, H, odd64)
        c01, c11 = swap(a1, b1, H, odd64)
        out_ref[0, 2 * p] = c00.astype(out_ref.dtype)
        out_ref[0, 2 * p + 1] = c01.astype(out_ref.dtype)
        out_ref[1, 2 * p] = c10.astype(out_ref.dtype)
        out_ref[1, 2 * p + 1] = c11.astype(out_ref.dtype)


def place_slots(arrived):
    groups, pairs, quarter, _ = arrived.shape
    step = 7
    return pl.pallas_call(
        place_kernel,
        grid=(pairs // step,),
        in_specs=[pl.BlockSpec((groups, step, quarter, T), lambda i: (0, i, 0, 0))],
        out_specs=pl.BlockSpec((CR1, 2 * step, quarter, T), lambda i: (0, i, 0, 0)),
        out_shape=jax.ShapeDtypeStruct((CR1, 2 * pairs, quarter, T), jnp.bfloat16),
        name="place_slots",
    )(arrived)


def per_device(
    a_diag, diag_cols, a_offd, offd_cols, prolong, aggregate, send_rows, ghost_agg, coarse_map
):
    me = lax.axis_index("rows").reshape(1)
    gathered, left, own, table, cols = gather_all(
        a_diag, diag_cols, a_offd, offd_cols, prolong, aggregate, send_rows
    )
    gathered = gathered.reshape(2 * NZ * NY, ROWS, T)
    offd = offd_terms(me, coarse_map[0], table, cols, left, gathered, own)
    return place_slots(swap_slices(offd))


def solution(mesh):
    in_specs = (
        P("rows", "grp", None, None),
        P("rows", "grp"),
        P("rows", "grp", None, None),
        P("rows", "grp"),
        P("rows", None, None, None),
        P("rows", None),
        P("rows", None, None),
        P("rows", None, None, None),
        P("rows", None),
    )
    out_specs = P("rows", None, "grp", None)
    return jax.shard_map(
        per_device, mesh=mesh, in_specs=in_specs, out_specs=out_specs, check_vma=False
    )
```

time: 99.1 us -> 91.4 us (0.922)
  blocking collectives: 29.4 us -> 0 us
  Pallas kernels: 59.6 us -> 83.7 us
  local copies, waits for them, and re-layouts: 9.76 us -> 7.2 us
    all_to_all x1 -> x0, blocking collectives: 29.4 us -> none  [per_device(): lax.all_to_all(offd, 'grp', split_axis=0, concat_axis=0, tiled=True)]
    pallas_call x3 -> x4, Pallas kernels: 59.6 us -> 83.7 us  [the longest x1 44.9 us: gather_all(): pl.pallas_call(gather_kernel, in_specs=[smem, smem, vmem, vmem, hbm, hbm,...]
    unnamed x14 -> x18, local copies, waits for them, and re-layouts: 9.66 us -> 7.2 us
where the time goes in v3:
time: 91.4 us; the launch traced here: 91 us
  Pallas kernels  83.7 us (92%)
  local copies, waits for them, and re-layouts  7.2 us (8%)
    pallas_call x1, Pallas kernels, gather_all(): pl.pallas_call(gather_kernel, in_specs=[smem, smem, vmem, vmem, hbm, hbm,...  44.9 us
    pallas_call x1, Pallas kernels, swap_slices(): pl.pallas_call(swap_kernel, in_specs=[vmem], out_specs=vmem, out_shape=ja...  21.7 us
    pallas_call x1, Pallas kernels, offd_terms(): pl.pallas_call(offd_kernel, in_specs=[smem, smem, smem, smem, vmem, vmem,...  10.9 us
    unnamed x18, local copies, waits for them, and re-layouts  7.2 us
    pallas_call x1, Pallas kernels, place_slots(): pl.pallas_call(place_kernel, grid=(pairs // step,), in_specs=[pl.BlockSpe...  6.19 us

profile of v3, /device:TPU:1, one launch (start us, length us, event | category | flops | bytes accessed | tf_op | source)
XLA Modules:
  0.0 91.0 jit_solution(10648369534447641319)
XLA Ops:
  0.0 0.0 copy-start.8
  0.0 0.0 copy-start.1
  0.0 1.1 %copy-done.1 = bf16[8,3,128,128]{3,2,1,0:T(8,128)(2,1)S(1)} copy-done((bf16[8,3,128,128]{3,2,1,0:T(8,128)(2,1)S(1)}, bf16[8,3,128,128]{3,2,1,0:T(8,128)(2,1)}, u32[]{:S(2)}) %copy-start.1) | copy-done | bytes 786456
  1.1 0.0 copy-start.2
  1.2 1.1 %copy-done.2 = bf16[8,3,128,128]{3,2,1,0:T(8,128)(2,1)S(1)} copy-done((bf16[8,3,128,128]{3,2,1,0:T(8,128)(2,1)S(1)}, bf16[8,3,128,128]{3,2,1,0:T(8,128)(2,1)}, u32[]{:S(2)}) %copy-start.2) | copy-done | bytes 786456
  2.3 0.0 copy-start.3
  2.3 1.0 %copy-done.3 = bf16[8,2,128,128]{3,2,1,0:T(8,128)(2,1)S(1)} copy-done((bf16[8,2,128,128]{3,2,1,0:T(8,128)(2,1)S(1)}, bf16[8,2,128,128]{3,2,1,0:T(8,128)(2,1)}, u32[]{:S(2)}) %copy-start.3) | copy-done | bytes 524312
  3.3 0.0 copy-start.4
  3.3 0.7 copy-done.4
  4.0 0.0 copy-start.5
  4.0 0.7 copy-done.5
  4.7 0.0 copy-start.6
  4.7 0.7 copy-done.6
  5.4 0.0 copy-start.7
  5.4 0.7 copy-done.7
  6.1 44.9 %gather_all.1 = (bf16[2,8,4,528,128]{4,3,2,1,0:T(8,128)(2,1)S(1)}, bf16[4,8,3,256,128]{4,3,2,1,0:T(8,128)(2,1)S(1)}, f32[128,128]{1,0:T(8,128)S(1)}, s32[64,128]{1,0:T(8,128)S(1)}, s32[4,8,128]{2,1,0:T(8,128)S(1)}) custom-call(s32[2,8]{1,0:T(2,128)S(1)} %bitcast.13, s32[3,8]{1,0:T(4,128)S(1)} %bitcast.10, s32[3,8]{1,0:T(4,128)S(1)} %bitcast.11, ...), custom_call_target="tpu_custom_call" | custom-call | tf_op jit(solution)/shard_map/gather_all/pallas_call | solution.py:366
  51.0 0.0 copy-done.8
  51.0 10.9 %offd_terms.1.src = bf16[4,49,32,128]{3,2,1,0:T(8,128)(2,1)S(1)} custom-call(s32[1]{0:T(128)} %bitcast.me_ref, s32[98]{0:T(128)S(1)} %bitcast.14, s32[64,128]{1,0:T(8,128)S(1)} %get-tuple-element.10.tbl_ref, s32[4,8,128]{2,1,0:T(8,128)S(1)} %get-tuple-element.11.cols_ref, bf16[4,8,3,256,128]{4,3,2,1,0:T(8,128)(2,1)S(1)} %get-tuple-element.12.l_ref, ...), custom_call_target="tpu_custom_call" | custom-call | tf_op jit(solution)/shard_map/offd_terms/pallas_call | solution.py:451
  61.9 21.7 %swap_slices.1.x_ref = bf16[4,49,32,128]{3,2,1,0:T(8,128)(2,1)S(1)} custom-call(bf16[4,49,32,128]{3,2,1,0:T(8,128)(2,1)S(1)} %offd_terms.1.src), custom_call_target="tpu_custom_call" | custom-call | tf_op jit(solution)/shard_map/swap_slices/pallas_call | solution.py:509
  83.6 0.0 copy-start
  83.6 1.2 %copy-done = bf16[4,49,32,128]{3,2,1,0:T(8,128)(2,1)} copy-done((bf16[4,49,32,128]{3,2,1,0:T(8,128)(2,1)}, bf16[4,49,32,128]{3,2,1,0:T(8,128)(2,1)S(1)}, u32[]{:S(2)}) %copy-start) | copy-done | bytes 1605656
  84.8 6.2 %place_slots.1 = bf16[2,98,32,128]{3,2,1,0:T(8,128)(2,1)} custom-call(bf16[4,49,32,128]{3,2,1,0:T(8,128)(2,1)} %copy-done), custom_call_target="tpu_custom_call" | custom-call | tf_op jit(solution)/shard_map/place_slots/pallas_call | solution.py:554
Async XLA Ops:
  0.0 51.0 %copy-start.8 = (s32[1,98]{1,0:T(1,128)S(1)}, s32[1,98]{1,0:T(1,128)}, u32[]{:S(2)}) copy-start(s32[1,98]{1,0:T(1,128)} %param.16) | copy-start | bytes 1180
  0.0 1.1 %copy-start.1 = (bf16[8,3,128,128]{3,2,1,0:T(8,128)(2,1)S(1)}, bf16[8,3,128,128]{3,2,1,0:T(8,128)(2,1)}, u32[]{:S(2)}) copy-start(bf16[8,3,128,128]{3,2,1,0:T(8,128)(2,1)} %ad_hbm.1) | copy-start | bytes 2359300
  1.1 1.1 %copy-start.2 = (bf16[8,3,128,128]{3,2,1,0:T(8,128)(2,1)S(1)}, bf16[8,3,128,128]{3,2,1,0:T(8,128)(2,1)}, u32[]{:S(2)}) copy-start(bf16[8,3,128,128]{3,2,1,0:T(8,128)(2,1)} %ao_hbm.1) | copy-start | bytes 2359300
  2.3 1.0 %copy-start.3 = (bf16[8,2,128,128]{3,2,1,0:T(8,128)(2,1)S(1)}, bf16[8,2,128,128]{3,2,1,0:T(8,128)(2,1)}, u32[]{:S(2)}) copy-start(bf16[8,2,128,128]{3,2,1,0:T(8,128)(2,1)} %p_hbm.1) | copy-start | bytes 1572868
  3.3 0.7 copy-start.4
  4.0 0.7 copy-start.5
  4.7 0.7 copy-start.6
  5.4 0.7 copy-start.7
  83.6 1.2 %copy-start = (bf16[4,49,32,128]{3,2,1,0:T(8,128)(2,1)}, bf16[4,49,32,128]{3,2,1,0:T(8,128)(2,1)S(1)}, u32[]{:S(2)}) copy-start(bf16[4,49,32,128]{3,2,1,0:T(8,128)(2,1)S(1)} %swap_slices.1.x_ref) | copy-start | bytes 4816900

commit v4 on v3

--- a/solution.py
+++ b/solution.py
@@ -397,7 +397,12 @@
             collective_id=0, has_side_effects=True, vmem_limit_bytes=32 << 20
         ),
         name="gather_all",
-    )(aggregate.T, diag_cols.T, offd_cols.T, send_rows[0].T, prolong, a_diag, a_offd)
+    )(
+        *(
+            pltpu.with_memory_space_constraint(item, pltpu.HBM)
+            for item in (aggregate.T, diag_cols.T, offd_cols.T, send_rows[0].T, prolong, a_diag, a_offd)
+        )
+    )
 
 
 def offd_kernel(me_ref, map_ref, tbl_ref, cols_ref, l_ref, gath_ref, d_ref, out_ref, acc):
@@ -422,7 +427,7 @@
             acc[slot] += jnp.where(high == odd, kept, pltpu.roll(moved, H, 1))
         return 0
 
-    lax.fori_loop(0, rows, row, 0)
+    lax.fori_loop(0, rows, row, 0, unroll=2)
     acc[slot_of(me_ref[0])] = d_ref[...]
 
     lane = lax.broadcasted_iota(jnp.int32, (T, T), 1)
@@ -440,7 +445,7 @@
             out_ref[g, p] = both[g * quarter : (g + 1) * quarter]
         return 0
 
-    lax.fori_loop(0, out_ref.shape[1], pack, 0)
+    lax.fori_loop(0, out_ref.shape[1], pack, 0, unroll=7)
 
 
 def offd_terms(me, col_map, table, cols, left, gathered, own):
@@ -459,49 +464,31 @@
     )(me, col_map, table, cols, left, gathered, own)
 
 
-def swap_kernel(src, out, hold, ssem, rsem, lsem):
+def swap_kernel(src, out, ssem, rsem, lsem):
     me = lax.axis_index("rows")
     x = lax.axis_index("grp")
     at = [lax.rem(x + d, 4) for d in range(4)]
-    up, down = (me, at[1]), (me, at[3])
     barrier = pltpu.get_barrier_semaphore()
-    for device in (up, down):
-        pl.semaphore_signal(barrier, inc=1, device_id=device, device_id_type=MESH)
-    pl.semaphore_wait(barrier, 2)
-    pairs = src.shape[1]
-    cut = pairs // 2
-    low, top = pl.ds(0, cut), pl.ds(cut, pairs - cut)
-
-    def remote(a, b, i, device):
-        return pltpu.make_async_remote_copy(
-            src_ref=a, dst_ref=b, send_sem=ssem.at[i], recv_sem=rsem.at[i],
-            device_id=device, device_id_type=MESH,
-        )
-
-    far = src.at[at[2]]
-    sends = [
-        remote(far.at[low], hold.at[low], 0, up),
-        remote(far.at[top], hold.at[top], 1, down),
-        remote(src.at[at[1]], out.at[x], 2, up),
-        remote(src.at[at[3]], out.at[x], 3, down),
-    ]
-    for copy in sends:
-        copy.start()
+    for d in (2, 1, 3):
+        pl.semaphore_signal(barrier, inc=1, device_id=(me, at[d]), device_id_type=MESH)
     stay = pltpu.make_async_copy(src.at[x], out.at[x], lsem)
     stay.start()
-    remote(hold.at[low], hold.at[low], 0, up).wait_recv()
-    sends.append(remote(hold.at[low], out.at[at[3], low], 4, up))
-    sends[-1].start()
-    remote(hold.at[top], hold.at[top], 1, down).wait_recv()
-    sends.append(remote(hold.at[top], out.at[at[1], top], 5, down))
-    sends[-1].start()
-    remote(out.at[at[3]], out.at[at[3]], 2, up).wait_recv()
-    remote(out.at[at[1]], out.at[at[1]], 3, down).wait_recv()
-    remote(out.at[at[2], low], out.at[at[2], low], 4, up).wait_recv()
-    remote(out.at[at[2], top], out.at[at[2], top], 5, down).wait_recv()
+    pl.semaphore_wait(barrier, 3)
+
+    def remote(d, a, b):
+        return pltpu.make_async_remote_copy(
+            src_ref=a, dst_ref=b, send_sem=ssem.at[d - 1], recv_sem=rsem.at[d - 1],
+            device_id=(me, at[d]), device_id_type=MESH,
+        )
+
+    for d in (2, 1, 3):
+        remote(d, src.at[at[d]], out.at[x]).start()
+    for d in (1, 3, 2):
+        came = out.at[at[4 - d]]
+        remote(d, came, came).wait_recv()
     stay.wait()
-    for copy in sends:
-        copy.wait_send()
+    for d in (1, 3, 2):
+        remote(d, src.at[at[d]], out.at[x]).wait_send()
 
 
 def swap_slices(src):
@@ -512,9 +499,8 @@
         out_specs=vmem,
         out_shape=jax.ShapeDtypeStruct(src.shape, src.dtype),
         scratch_shapes=[
-            pltpu.VMEM(src.shape[1:], src.dtype),
-            pltpu.SemaphoreType.DMA((6,)),
-            pltpu.SemaphoreType.DMA((6,)),
+            pltpu.SemaphoreType.DMA((3,)),
+            pltpu.SemaphoreType.DMA((3,)),
             pltpu.SemaphoreType.DMA,
         ],
         compiler_params=pltpu.CompilerParams(
@@ -524,39 +510,44 @@
     )(src)
 
 
-def place_kernel(x_ref, out_ref):
+def place_kernel(x_ref, out_hbm, buf, sem):
     pairs, quarter = x_ref.shape[1], x_ref.shape[2]
-    lane = lax.broadcasted_iota(jnp.int32, (quarter, T), 1)
-    odd32 = lax.rem(lane // 32, 2) == 1
-    odd64 = lane >= H
-
-    def swap(a, b, shift, odd):
-        return (
-            jnp.where(odd, pltpu.roll(b, shift, 1), a),
-            jnp.where(odd, b, pltpu.roll(a, T - shift, 1)),
-        )
-
-    for p in range(pairs):
-        w = [x_ref[s, p].astype(jnp.float32) for s in range(4)]
-        a0, a1 = swap(w[0], w[1], 32, odd32)
-        b0, b1 = swap(w[2], w[3], 32, odd32)
-        c00, c10 = swap(a0, b0, H, odd64)
-        c01, c11 = swap(a1, b1, H, odd64)
-        out_ref[0, 2 * p] = c00.astype(out_ref.dtype)
-        out_ref[0, 2 * p + 1] = c01.astype(out_ref.dtype)
-        out_ref[1, 2 * p] = c10.astype(out_ref.dtype)
-        out_ref[1, 2 * p + 1] = c11.astype(out_ref.dtype)
+    chunks = sem.shape[1]
+    step = pairs // chunks
+
+    def copies(n):
+        at = pl.ds(2 * step * n, 2 * step)
+        return [pltpu.make_async_copy(buf.at[r, at], out_hbm.at[r, at], sem.at[r, n]) for r in range(CR1)]
+
+    row = lax.broadcasted_iota(jnp.int32, (4 * T, 4 * T), 0)
+    col = lax.broadcasted_iota(jnp.int32, (4 * T, 4 * T), 1)
+    move = (row % 32 == col % 32) & ((row // 32) % 4 == col // T) & (row // T == (col // 32) % 4)
+    move = jnp.where(move, 1.0, 0.0).astype(jnp.bfloat16)
+    for n in range(chunks):
+        at = pl.ds(n * step, step)
+        x = jnp.concatenate([x_ref[s, at].reshape(step * quarter, T) for s in range(4)], axis=1)
+        o = jnp.dot(x, move, preferred_element_type=jnp.float32).astype(buf.dtype)
+        for r in range(CR1):
+            for j in range(2):
+                piece = o[:, (r * 2 + j) * T : (r * 2 + j + 1) * T].reshape(step, quarter, T)
+                for p in range(step):
+                    buf[r, 2 * (n * step + p) + j] = piece[p]
+        for copy in copies(n):
+            copy.start()
+    for n in range(chunks):
+        for copy in copies(n):
+            copy.wait()
 
 
 def place_slots(arrived):
     groups, pairs, quarter, _ = arrived.shape
-    step = 7
+    shape = (CR1, 2 * pairs, quarter, T)
     return pl.pallas_call(
         place_kernel,
-        grid=(pairs // step,),
-        in_specs=[pl.BlockSpec((groups, step, quarter, T), lambda i: (0, i, 0, 0))],
-        out_specs=pl.BlockSpec((CR1, 2 * step, quarter, T), lambda i: (0, i, 0, 0)),
-        out_shape=jax.ShapeDtypeStruct((CR1, 2 * pairs, quarter, T), jnp.bfloat16),
+        in_specs=[pl.BlockSpec(memory_space=pltpu.VMEM)],
+        out_specs=pl.BlockSpec(memory_space=pltpu.HBM),
+        out_shape=jax.ShapeDtypeStruct(shape, jnp.bfloat16),
+        scratch_shapes=[pltpu.VMEM(shape, jnp.bfloat16), pltpu.SemaphoreType.DMA((CR1, 7))],
         name="place_slots",
     )(arrived)
 

time: 91.4 us -> 78.6 us (0.86)
  Pallas kernels: 83.7 us -> 77.2 us
  local copies, waits for them, and re-layouts: 7.2 us -> 1.17 us
    unnamed x18 -> x4, local copies, waits for them, and re-layouts: 7.2 us -> 1.17 us
    pallas_call x1, Pallas kernels: 10.9 us -> 6.7 us  [offd_terms(): pl.pallas_call(offd_kernel, in_specs=[smem, smem, smem, smem, vmem, vmem,...]
    pallas_call x1, Pallas kernels: 6.19 us -> 3.28 us  [place_slots(): pl.pallas_call(place_kernel, in_specs=[pl.BlockSpec(memory_space=pltpu.VM...]
where the time goes in v4:
time: 78.6 us; the launch traced here: 78.4 us
  Pallas kernels  77.2 us (98%)
  local copies, waits for them, and re-layouts  1.17 us (1%)
    pallas_call x1, Pallas kernels, gather_all(): pl.pallas_call(gather_kernel, in_specs=[smem, smem, vmem, vmem, hbm, hbm,...  45.2 us
    pallas_call x1, Pallas kernels, swap_slices(): pl.pallas_call(swap_kernel, in_specs=[vmem], out_specs=vmem, out_shape=ja...  22.1 us
    pallas_call x1, Pallas kernels, offd_terms(): pl.pallas_call(offd_kernel, in_specs=[smem, smem, smem, smem, vmem, vmem,...  6.7 us
    pallas_call x1, Pallas kernels, place_slots(): pl.pallas_call(place_kernel, in_specs=[pl.BlockSpec(memory_space=pltpu.VM...  3.28 us

profile of v4, /device:TPU:1, one launch (start us, length us, event | category | flops | bytes accessed | tf_op | source)
XLA Modules:
  0.0 78.4 jit_solution(740723252406301804)
XLA Ops:
  0.0 0.0 copy-start.1
  0.0 45.2 %gather_all.1 = (bf16[2,8,4,528,128]{4,3,2,1,0:T(8,128)(2,1)S(1)}, bf16[4,8,3,256,128]{4,3,2,1,0:T(8,128)(2,1)S(1)}, f32[128,128]{1,0:T(8,128)S(1)}, s32[64,128]{1,0:T(8,128)S(1)}, s32[4,8,128]{2,1,0:T(8,128)S(1)}) custom-call(s32[2,8]{1,0:T(2,128)} %bitcast.14, s32[3,8]{1,0:T(4,128)} %bitcast.11, s32[3,8]{1,0:T(4,128)} %bitcast.12, s32[4,64]{1,0:T(4,128)} %bitcast.13, ...), custom_call_target="tpu_custom_call" | custom-call | tf_op jit(solution)/shard_map/gather_all/pallas_call | solution.py:366
  45.2 0.0 copy-done.1
  45.2 6.7 %offd_terms.1.src = bf16[4,49,32,128]{3,2,1,0:T(8,128)(2,1)S(1)} custom-call(s32[1]{0:T(128)} %bitcast.me_ref, s32[98]{0:T(128)S(1)} %bitcast.10, s32[64,128]{1,0:T(8,128)S(1)} %get-tuple-element.10.tbl_ref, s32[4,8,128]{2,1,0:T(8,128)S(1)} %get-tuple-element.11.cols_ref, bf16[4,8,3,256,128]{4,3,2,1,0:T(8,128)(2,1)S(1)} %get-tuple-element.12.l_ref, ...), custom_call_target="tpu_custom_call" | custom-call | tf_op jit(solution)/shard_map/offd_terms/pallas_call | solution.py:456
  51.9 22.1 %swap_slices.1.x_ref = bf16[4,49,32,128]{3,2,1,0:T(8,128)(2,1)S(1)} custom-call(bf16[4,49,32,128]{3,2,1,0:T(8,128)(2,1)S(1)} %offd_terms.1.src), custom_call_target="tpu_custom_call" | custom-call | tf_op jit(solution)/shard_map/swap_slices/pallas_call | solution.py:496
  74.0 0.0 copy-start
  74.0 1.2 %copy-done = bf16[4,49,32,128]{3,2,1,0:T(8,128)(2,1)} copy-done((bf16[4,49,32,128]{3,2,1,0:T(8,128)(2,1)}, bf16[4,49,32,128]{3,2,1,0:T(8,128)(2,1)S(1)}, u32[]{:S(2)}) %copy-start) | copy-done | bytes 1605656
  75.1 3.3 %place_slots.1 = bf16[2,98,32,128]{3,2,1,0:T(8,128)(2,1)} custom-call(bf16[4,49,32,128]{3,2,1,0:T(8,128)(2,1)} %copy-done), custom_call_target="tpu_custom_call" | custom-call | tf_op jit(solution)/shard_map/place_slots/pallas_call | solution.py:545
Async XLA Ops:
  0.0 45.2 %copy-start.1 = (s32[1,98]{1,0:T(1,128)S(1)}, s32[1,98]{1,0:T(1,128)}, u32[]{:S(2)}) copy-start(s32[1,98]{1,0:T(1,128)} %param.16) | copy-start | bytes 1180
  74.0 1.2 %copy-start = (bf16[4,49,32,128]{3,2,1,0:T(8,128)(2,1)}, bf16[4,49,32,128]{3,2,1,0:T(8,128)(2,1)S(1)}, u32[]{:S(2)}) copy-start(bf16[4,49,32,128]{3,2,1,0:T(8,128)(2,1)S(1)} %swap_slices.1.x_ref) | copy-start | bytes 4816900

commit v5 on v4

--- a/solution.py
+++ b/solution.py
@@ -16,8 +16,7 @@
 ZR = 320
 NZ, NY = 8, 4
 MESH = pl.DeviceIdType.MESH
-PARTS = {"z": (0, ZR), "za": (0, ZR // 2), "zb": (ZR // 2, ZR // 2),
-         "y": (ZR, ROWS - ZR), "ya": (ZR, 112), "yb": (ZR + 112, ROWS - ZR - 112)}
+PARTS = {"z": (0, ZR), "za": (0, ZR // 2), "zb": (ZR // 2, ZR // 2), "y": (ZR, ROWS - ZR)}
 DZ = (0, 1, -1, 2, -2, 3, -3, 4)
 LATE_UP = (0, 1, 2, 3)
 
@@ -25,58 +24,73 @@
 def flood_plan():
     plan = {}
 
-    def add(name, link, there, here, part, after):
-        plan[name] = (link, there, here, part, tuple(after))
-
-    for sign, link in ((1, "z+"), (-1, "z-")):
-        for d in range(1, 5):
-            part = "z" if d < 4 else ("za" if sign == 1 else "zb")
-            after = [] if d == 1 else [("Z", sign * (d - 1))]
-            here = sign * d if d < 4 else 4
-            name = ("Z", here) if d < 4 else ("Z", 4, sign)
-            add(name, link, (sign * (d - 1), 0), (here, 0), part, after)
+    def add(name, way, there, here, part, after):
+        plan[name] = (way, there, here, part, tuple(after))
+
+    for s in (1, -1):
+        add(("Z", s), ("z", s), (0, 0), (s, 0), "z", [])
+        add(("Z", 2 * s), ("z", 2 * s), (0, 0), (2 * s, 0), "z", [])
+        add(("Z", 3 * s), ("z", s), (2 * s, 0), (3 * s, 0), "z", [("Z", 2 * s)])
+        add(("Z", 4, s), ("z", 2 * s), (2 * s, 0), (4, 0), "za" if s == 1 else "zb", [("Z", 2 * s)])
+        add(("Y", s), ("y", s), (0, 0), (0, s), "y", [])
+    add(("Y", 2), ("y", 2), (0, 0), (0, 2), "y", [])
     for e in DZ:
         have = [] if e == 0 else ([("Z", e)] if e != 4 else [("Z", 4, 1), ("Z", 4, -1)])
-        for sign, link in ((1, "y+"), (-1, "y-")):
-            add(("ZY", e, sign), link, (e, 0), (e, sign), "z", have)
-        sign = 1 if e in LATE_UP else -1
-        add(("ZY", e, 2), "y+" if sign == 1 else "y-", (e, sign), (e, 2), "z", [("ZY", e, sign)])
-    for sign, link in ((1, "y+"), (-1, "y-")):
-        add(("Y", sign), link, (0, 0), (0, sign), "y", [])
-        add(("Y", 2, sign), link, (0, sign), (0, 2), "ya" if sign == 1 else "yb", [("Y", sign)])
-    for sign, link in ((1, "z+"), (-1, "z-")):
+        for s in (1, -1):
+            add(("ZY", e, s), ("y", s), (e, 0), (e, s), "z", have)
+        s = 1 if e in LATE_UP else -1
+        add(("ZY", e, 2), ("y", s), (e, s), (e, 2), "z", [("ZY", e, s)])
+    for s in (1, -1):
         for d in range(1, 5):
             for dy in (0, 1, -1, 2):
-                if d == 4 and (dy in (0, 1)) != (sign == 1):
+                if d == 4 and (dy in (0, 1)) != (s == 1):
                     continue
                 if d > 1:
-                    after = [("YZ", sign * (d - 1), dy)]
-                elif dy == 0:
-                    after = []
+                    after = [("YZ", s * (d - 1), dy)]
                 else:
-                    after = [("Y", dy)] if dy != 2 else [("Y", 2, 1), ("Y", 2, -1)]
-                here = sign * d if d < 4 else 4
-                add(("YZ", here, dy), link, (sign * (d - 1), dy), (here, dy), "y", after)
+                    after = [("Y", dy)] if dy else []
+                here = s * d if d < 4 else 4
+                add(("YZ", here, dy), ("z", s), (s * (d - 1), dy), (here, dy), "y", after)
     return plan
 
 
-def flood_order(plan):
+def flood_rank(plan):
+    kids = {}
+    for name, item in plan.items():
+        for a in item[4]:
+            kids.setdefault(a, []).append(name)
+    memo = {}
+
+    def depth(name):
+        if name not in memo:
+            memo[name] = 1 + max([depth(k) for k in kids.get(name, [])], default=0)
+        return memo[name]
+
+    kind = {"Y": 0, "Z": 1, "YZ": 2, "ZY": 3}
+    return {n: (-depth(n), kind[n[0]], abs(n[1]), str(n)) for n in plan}
+
+
+def flood_order(plan, latency=2.5, rate=49e3):
+    rank = flood_rank(plan)
     free = {}
     arrive, waiting = {}, dict(plan)
-    rank = {"Y": 0, "Z": 1, "YZ": 2, "ZY": 3}
-    while len(arrive) < len(plan):
+    while waiting:
         best = None
-        for name, (link, _, _, part, after) in waiting.items():
+        for name, ((axis, hop), _, _, part, after) in waiting.items():
             if any(a not in arrive for a in after):
                 continue
-            start = max([arrive[a] for a in after] + [free.get(link, 0.0)])
-            key = (start, rank[name[0]], abs(name[1]), str(name))
+            if axis == "y" and hop == 2:
+                links = ((("y", 1), 1), (("y", -1), 1))
+            else:
+                links = (((axis, 1 if hop > 0 else -1), abs(hop)),)
+            start = max([arrive[a] for a in after] + [free.get(link, 0.0) for link, _ in links])
+            key = (start,) + rank[name]
             if best is None or key < best[0]:
-                best = (key, name, start, link, part)
-        _, name, start, link, part = best
-        end = start + PARTS[part][1] * 256 / 50e3
-        free[link] = end
-        arrive[name] = end + 1.5
+                best = (key, name, start, links, PARTS[part][1] * 256 / rate)
+        _, name, start, links, took = best
+        for link, hops in links:
+            free[link] = start + hops * took
+        arrive[name] = start + took + latency
         del waiting[name]
     return arrive
 
@@ -96,19 +110,11 @@
     def row_of(zz, yy, cc):
         return (zz * NY + yy) * 2 + cc
 
-    up_z, dn_z = lax.rem(z + 1, NZ), lax.rem(z + NZ - 1, NZ)
-    up_y, dn_y = lax.rem(y + 1, NY), lax.rem(y + NY - 1, NY)
     xat = [lax.rem(x + d, 4) for d in range(4)]
-    link_to = {
-        "z+": (row_of(up_z, y, core), x),
-        "z-": (row_of(dn_z, y, core), x),
-        "y+": (row_of(z, up_y, core), x),
-        "y-": (row_of(z, dn_y, core), x),
-        "core": (row_of(z, y, 1 - core), x),
-        1: (me, xat[1]),
-        2: (me, xat[2]),
-        3: (me, xat[3]),
-    }
+    link_to = {("z", d): (row_of(lax.rem(z + (NZ + d), NZ), y, core), x) for d in (1, -1, 2, -2)}
+    link_to.update({("y", d): (row_of(z, lax.rem(y + (NY + d), NY), core), x) for d in (1, -1, 2)})
+    link_to["core"] = (row_of(z, y, 1 - core), x)
+    link_to.update({d: (me, xat[d]) for d in (1, 2, 3)})
     barrier = pltpu.get_barrier_semaphore()
     for device in link_to.values():
         pl.semaphore_signal(barrier, inc=1, device_id=device, device_id_type=MESH)
@@ -129,24 +135,12 @@
         )
 
     half = ao_hbm.shape[0] // 2
-    first, second = pl.ds(0, half), pl.ds(half, half)
-    a_plan = {
-        ("r", 0): (0, 1, first, 1), ("r", 1): (0, 1, second, 1), ("r", 2): (1, 2, first, 1),
-        ("l", 1): (0, 3, second, 3), ("l", 0): (0, 3, first, 3), ("l", 2): (3, 2, second, 3),
-    }
-    a_index = {name: i for i, name in enumerate(a_plan)}
-
-    def a_copy(name, sending):
-        src_slot, dst_slot, part, to = a_plan[name]
-        dst = a_all.at[dst_slot, part]
-        src = (ao_hbm if src_slot == 0 else a_all.at[src_slot]).at[part] if sending else dst
-        i = a_index[name]
-        return remote(src, dst, xs_sem.at[i], xr_sem.at[i], link_to[to])
-
-    def a_send(name):
-        copy = a_copy(name, True)
-        copy.start()
-        sends.append(copy)
+
+    def a_copy(d, part, sending):
+        at = pl.ds(part * half, half)
+        dst = a_all.at[d, at]
+        i = 2 * (d - 1) + part
+        return remote(ao_hbm.at[at] if sending else dst, dst, xs_sem.at[i], xr_sem.at[i], link_to[d])
 
     def c_copy(d):
         return remote(ctab.at[0], ctab.at[d], xs_sem.at[5 + d], xr_sem.at[5 + d], link_to[d])
@@ -190,9 +184,10 @@
 
     started = set()
 
+    rank = flood_rank(plan)
+
     def start_ready(have):
-        order = {"Y": 0, "Z": 1, "YZ": 2, "ZY": 3}
-        for name in sorted(plan, key=lambda n: (order[n[0]], abs(n[1]), str(n))):
+        for name in sorted(plan, key=rank.get):
             if name not in started and all(a in have for a in plan[name][4]):
                 started.add(name)
                 copy = f_copy(name, True)
@@ -210,7 +205,7 @@
         zs = [] if dz == 0 else ([("Z", dz)] if dz != 4 else [("Z", 4, 1), ("Z", 4, -1)])
         need[("z", dz)] = zs + [("ZY", dz, s) for s in (1, -1, 2)]
         need[("y", dz)] = (
-            [("Y", 1), ("Y", -1), ("Y", 2, 1), ("Y", 2, -1)]
+            [("Y", 1), ("Y", -1), ("Y", 2)]
             if dz == 0
             else [("YZ", dz, s) for s in (0, 1, -1, 2)]
         )
@@ -226,8 +221,10 @@
     pl.semaphore_wait(barrier, len(link_to))
     have = set()
     start_ready(have)
-    for name in (("r", 0), ("l", 1), ("r", 1), ("l", 0)):
-        a_send(name)
+    for d, part in ((1, 0), (3, 0), (2, 0), (2, 1), (1, 1), (3, 1)):
+        copy = a_copy(d, part, True)
+        copy.start()
+        sends.append(copy)
     for d in (1, 2, 3):
         copy = c_copy(d)
         copy.start()
@@ -294,10 +291,9 @@
             copy.start()
             sends.append(copy)
 
-    def a_take(name, then=None):
-        a_copy(name, False).wait_recv()
-        if then:
-            a_send(then)
+    def a_take(d, part):
+        a_copy(d, part, False).wait_recv()
+        left_rows(d, part)
 
     def begin():
         dacc[...] = jnp.zeros_like(dacc)
@@ -310,11 +306,9 @@
         (0.0, begin), (1.5, lambda: diag_rows(0, 2)), (3.5, lambda: diag_rows(2, 4)),
         (5.5, lambda: diag_rows(4, 6)), (7.5, lambda: diag_rows(6, 8)),
         (7.6, send_diag),
-        (9.5, lambda: a_take(("r", 0), ("r", 2))), (9.6, lambda: a_take(("l", 1), ("l", 2))),
         (10.5, lambda: left_rows(0, 0)), (12.0, lambda: left_rows(0, 1)),
-        (13.5, lambda: left_rows(1, 0)), (15.0, lambda: left_rows(3, 1)),
-        (18.0, lambda: (a_take(("r", 1)), left_rows(1, 1))),
-        (19.5, lambda: (a_take(("l", 0)), left_rows(3, 0))),
+        (17.0, lambda: a_take(1, 0)), (19.0, lambda: a_take(3, 0)),
+        (22.0, lambda: a_take(2, 0)), (24.0, lambda: a_take(2, 1)),
     ]
     events += [(t, 0, step) for t, step in steps]
     kept = False
@@ -329,9 +323,8 @@
             kept = True
             keep.wait()
         share(have)
-    for name, part in ((("r", 2), 0), (("l", 2), 1)):
-        a_take(name)
-        left_rows(2, part)
+    a_take(1, 1)
+    a_take(3, 1)
 
     total = dsend[x]
     for d in (1, 2, 3):
@@ -548,6 +541,7 @@
         out_specs=pl.BlockSpec(memory_space=pltpu.HBM),
         out_shape=jax.ShapeDtypeStruct(shape, jnp.bfloat16),
         scratch_shapes=[pltpu.VMEM(shape, jnp.bfloat16), pltpu.SemaphoreType.DMA((CR1, 7))],
+        compiler_params=pltpu.CompilerParams(vmem_limit_bytes=16 << 20),
         name="place_slots",
     )(arrived)
 

time: 78.6 us -> 79.6 us (1.013)
  Pallas kernels: 77.2 us -> 79.5 us
  local copies, waits for them, and re-layouts: 1.17 us -> 0.01 us
    pallas_call x1, Pallas kernels: 45.2 us -> 50 us  [gather_all(): pl.pallas_call(gather_kernel, in_specs=[smem, smem, vmem, vmem, hbm, hbm,...]
    pallas_call x1, Pallas kernels: 3.28 us -> 1.86 us  [place_slots(): pl.pallas_call(place_kernel, in_specs=[pl.BlockSpec(memory_space=pltpu.VM...]
    unnamed x4 -> x2, local copies, waits for them, and re-layouts: 1.17 us -> 0.01 us
    pallas_call x1, Pallas kernels: 22.1 us -> 20.9 us  [swap_slices(): pl.pallas_call(swap_kernel, in_specs=[vmem], out_specs=vmem, out_shape=ja...]
where the time goes in v5:
time: 79.6 us; the launch traced here: 79.5 us
  Pallas kernels  79.5 us (100%)
    pallas_call x1, Pallas kernels, gather_all(): pl.pallas_call(gather_kernel, in_specs=[smem, smem, vmem, vmem, hbm, hbm,...  50 us
    pallas_call x1, Pallas kernels, swap_slices(): pl.pallas_call(swap_kernel, in_specs=[vmem], out_specs=vmem, out_shape=ja...  20.9 us
    pallas_call x1, Pallas kernels, offd_terms(): pl.pallas_call(offd_kernel, in_specs=[smem, smem, smem, smem, vmem, vmem,...  6.69 us
    pallas_call x1, Pallas kernels, place_slots(): pl.pallas_call(place_kernel, in_specs=[pl.BlockSpec(memory_space=pltpu.VM...  1.86 us

profile of v5, /device:TPU:1, one launch (start us, length us, event | category | flops | bytes accessed | tf_op | source)
XLA Modules:
  0.0 79.5 jit_solution(4184523307416733380)
XLA Ops:
  0.0 0.0 copy-start
  0.0 50.0 %gather_all.1 = (bf16[2,8,4,528,128]{4,3,2,1,0:T(8,128)(2,1)S(1)}, bf16[4,8,3,256,128]{4,3,2,1,0:T(8,128)(2,1)S(1)}, f32[128,128]{1,0:T(8,128)S(1)}, s32[64,128]{1,0:T(8,128)S(1)}, s32[4,8,128]{2,1,0:T(8,128)S(1)}) custom-call(s32[2,8]{1,0:T(2,128)} %bitcast.14, s32[3,8]{1,0:T(4,128)} %bitcast.11, s32[3,8]{1,0:T(4,128)} %bitcast.12, s32[4,64]{1,0:T(4,128)} %bitcast.13, ...), custom_call_target="tpu_custom_call" | custom-call | tf_op jit(solution)/shard_map/gather_all/pallas_call | solution.py:359
  50.0 0.0 copy-done
  50.0 6.7 %offd_terms.1.src = bf16[4,49,32,128]{3,2,1,0:T(8,128)(2,1)S(1)} custom-call(s32[1]{0:T(128)} %bitcast.me_ref, s32[98]{0:T(128)S(1)} %bitcast.10, s32[64,128]{1,0:T(8,128)S(1)} %get-tuple-element.10.tbl_ref, s32[4,8,128]{2,1,0:T(8,128)S(1)} %get-tuple-element.11.cols_ref, bf16[4,8,3,256,128]{4,3,2,1,0:T(8,128)(2,1)S(1)} %get-tuple-element.12.l_ref, ...), custom_call_target="tpu_custom_call" | custom-call | tf_op jit(solution)/shard_map/offd_terms/pallas_call | solution.py:449
  56.7 20.9 %swap_slices.1.x_ref = bf16[4,49,32,128]{3,2,1,0:T(8,128)(2,1)S(1)} custom-call(bf16[4,49,32,128]{3,2,1,0:T(8,128)(2,1)S(1)} %offd_terms.1.src), custom_call_target="tpu_custom_call" | custom-call | tf_op jit(solution)/shard_map/swap_slices/pallas_call | solution.py:489
  77.7 1.9 %place_slots.1 = bf16[2,98,32,128]{3,2,1,0:T(8,128)(2,1)} custom-call(bf16[4,49,32,128]{3,2,1,0:T(8,128)(2,1)S(1)} %swap_slices.1.x_ref), custom_call_target="tpu_custom_call" | custom-call | tf_op jit(solution)/shard_map/place_slots/pallas_call | solution.py:538
Async XLA Ops:
  0.0 50.0 %copy-start = (s32[1,98]{1,0:T(1,128)S(1)}, s32[1,98]{1,0:T(1,128)}, u32[]{:S(2)}) copy-start(s32[1,98]{1,0:T(1,128)} %param.16) | copy-start | bytes 1180

commit v6 on v4

--- a/solution.py
+++ b/solution.py
@@ -156,6 +156,9 @@
     stage[...] = jnp.zeros_like(stage)
     stage[0 : srows_ref.shape[0], 0 : srows_ref.shape[1]] = srows_ref[...].astype(jnp.float32)
     ctab[0, 0 : ocols_ref.shape[0], 0 : ocols_ref.shape[1]] = ocols_ref[...]
+    pl.semaphore_wait(barrier, len(link_to))
+    for name in (("r", 0), ("l", 1), ("r", 1), ("l", 0)):
+        a_send(name)
     loads[0].wait()
 
     def tile(i, a):
@@ -223,11 +226,8 @@
                 sends.append(copy)
                 del need[key]
 
-    pl.semaphore_wait(barrier, len(link_to))
     have = set()
     start_ready(have)
-    for name in (("r", 0), ("l", 1), ("r", 1), ("l", 0)):
-        a_send(name)
     for d in (1, 2, 3):
         copy = c_copy(d)
         copy.start()
@@ -405,13 +405,14 @@
     )
 
 
-def offd_kernel(me_ref, map_ref, tbl_ref, cols_ref, l_ref, gath_ref, d_ref, out_ref, acc):
+def slot_of(node):
+    return lax.rem(node, 2) * (NZ * NY) + node // 2
+
+
+def offd_kernel(me_ref, tbl_ref, cols_ref, l_ref, gath_ref, d_ref, acc):
     groups, rows, per, _, _ = l_ref.shape
     high = lax.broadcasted_iota(jnp.int32, (T, T), 1) >= H
     acc[...] = jnp.zeros_like(acc)
-
-    def slot_of(node):
-        return lax.rem(node, 2) * (NZ * NY) + node // 2
 
     def row(i, _):
         for t in range(groups * per):
@@ -430,84 +431,91 @@
     lax.fori_loop(0, rows, row, 0, unroll=2)
     acc[slot_of(me_ref[0])] = d_ref[...]
 
-    lane = lax.broadcasted_iota(jnp.int32, (T, T), 1)
-    even = lax.rem(lane // 32, 2) == 0
-
-    def pack(p, _):
-        def part(j):
-            gid = map_ref[2 * p + j]
-            shift = lax.rem((j - lax.rem(gid, CR1)) * 32 + T, T)
-            return pltpu.roll(acc[slot_of(gid // CR1)], shift, 1)
-
-        both = jnp.where(even, part(0), part(1)).astype(out_ref.dtype)
-        quarter = out_ref.shape[2]
-        for g in range(out_ref.shape[0]):
-            out_ref[g, p] = both[g * quarter : (g + 1) * quarter]
-        return 0
-
-    lax.fori_loop(0, out_ref.shape[1], pack, 0, unroll=7)
-
-
-def offd_terms(me, col_map, table, cols, left, gathered, own):
-    groups, rows, per, _, _ = left.shape
-    nodes = gathered.shape[0]
+
+def offd_terms(me, table, cols, left, gathered, own):
     vmem = pl.BlockSpec(memory_space=pltpu.VMEM)
     smem = pl.BlockSpec(memory_space=pltpu.SMEM)
     return pl.pallas_call(
         offd_kernel,
-        in_specs=[smem, smem, smem, smem, vmem, vmem, vmem],
+        in_specs=[smem, smem, smem, vmem, vmem, vmem],
         out_specs=vmem,
-        out_shape=jax.ShapeDtypeStruct((groups, col_map.shape[0] // 2, T // groups, T), jnp.bfloat16),
-        scratch_shapes=[pltpu.VMEM((nodes, T, T), jnp.float32)],
+        out_shape=jax.ShapeDtypeStruct((gathered.shape[0], T, T), jnp.float32),
         compiler_params=pltpu.CompilerParams(vmem_limit_bytes=32 << 20),
         name="offd_terms",
-    )(me, col_map, table, cols, left, gathered, own)
-
-
-def swap_kernel(src, out, ssem, rsem, lsem):
+    )(me, table, cols, left, gathered, own)
+
+
+def swap_kernel(map_ref, acc, out, src, ssem, rsem, lsem):
     me = lax.axis_index("rows")
     x = lax.axis_index("grp")
     at = [lax.rem(x + d, 4) for d in range(4)]
     barrier = pltpu.get_barrier_semaphore()
     for d in (2, 1, 3):
         pl.semaphore_signal(barrier, inc=1, device_id=(me, at[d]), device_id_type=MESH)
+    pairs, quarter = src.shape[1], src.shape[2]
+    chunks = ssem.shape[1]
+    step = pairs // chunks
+
+    lane = lax.broadcasted_iota(jnp.int32, (T, T), 1)
+    even = lax.rem(lane // 32, 2) == 0
+
+    def pack(p):
+        def part(j):
+            gid = map_ref[2 * p + j]
+            value = acc[slot_of(gid // CR1)]
+            return jnp.where(lax.rem(gid, CR1) == j, value, pltpu.roll(value, 32 if j else T - 32, 1))
+
+        both = jnp.where(even, part(0), part(1)).astype(src.dtype)
+        for g in range(src.shape[0]):
+            src[g, p] = both[g * quarter : (g + 1) * quarter]
+
+    def remote(d, c, a, b):
+        piece = pl.ds(c * step, step)
+        return pltpu.make_async_remote_copy(
+            src_ref=a.at[piece], dst_ref=b.at[piece],
+            send_sem=ssem.at[d - 1, c], recv_sem=rsem.at[d - 1, c],
+            device_id=(me, at[d]), device_id_type=MESH,
+        )
+
+    for c in range(chunks):
+        for p in range(c * step, (c + 1) * step):
+            pack(p)
+        if c == 0:
+            pl.semaphore_wait(barrier, 3)
+        for d in (2, 1, 3):
+            remote(d, c, src.at[at[d]], out.at[x]).start()
     stay = pltpu.make_async_copy(src.at[x], out.at[x], lsem)
     stay.start()
-    pl.semaphore_wait(barrier, 3)
-
-    def remote(d, a, b):
-        return pltpu.make_async_remote_copy(
-            src_ref=a, dst_ref=b, send_sem=ssem.at[d - 1], recv_sem=rsem.at[d - 1],
-            device_id=(me, at[d]), device_id_type=MESH,
-        )
-
-    for d in (2, 1, 3):
-        remote(d, src.at[at[d]], out.at[x]).start()
-    for d in (1, 3, 2):
-        came = out.at[at[4 - d]]
-        remote(d, came, came).wait_recv()
+    for c in range(chunks):
+        for d in (1, 3, 2):
+            came = out.at[at[4 - d]]
+            remote(d, c, came, came).wait_recv()
     stay.wait()
-    for d in (1, 3, 2):
-        remote(d, src.at[at[d]], out.at[x]).wait_send()
-
-
-def swap_slices(src):
+    for c in range(chunks):
+        for d in (1, 3, 2):
+            remote(d, c, src.at[at[d]], out.at[x]).wait_send()
+
+
+def swap_slices(col_map, sums):
     vmem = pl.BlockSpec(memory_space=pltpu.VMEM)
+    shape = (4, col_map.shape[0] // 2, T // 4, T)
+    chunks = 7
     return pl.pallas_call(
         swap_kernel,
-        in_specs=[vmem],
+        in_specs=[pl.BlockSpec(memory_space=pltpu.SMEM), vmem],
         out_specs=vmem,
-        out_shape=jax.ShapeDtypeStruct(src.shape, src.dtype),
+        out_shape=jax.ShapeDtypeStruct(shape, jnp.bfloat16),
         scratch_shapes=[
-            pltpu.SemaphoreType.DMA((3,)),
-            pltpu.SemaphoreType.DMA((3,)),
+            pltpu.VMEM(shape, jnp.bfloat16),
+            pltpu.SemaphoreType.DMA((3, chunks)),
+            pltpu.SemaphoreType.DMA((3, chunks)),
             pltpu.SemaphoreType.DMA,
         ],
         compiler_params=pltpu.CompilerParams(
             collective_id=1, has_side_effects=True, vmem_limit_bytes=16 << 20
         ),
         name="swap_slices",
-    )(src)
+    )(col_map, sums)
 
 
 def place_kernel(x_ref, out_hbm, buf, sem):
@@ -548,6 +556,7 @@
         out_specs=pl.BlockSpec(memory_space=pltpu.HBM),
         out_shape=jax.ShapeDtypeStruct(shape, jnp.bfloat16),
         scratch_shapes=[pltpu.VMEM(shape, jnp.bfloat16), pltpu.SemaphoreType.DMA((CR1, 7))],
+        compiler_params=pltpu.CompilerParams(vmem_limit_bytes=16 << 20),
         name="place_slots",
     )(arrived)
 
@@ -560,8 +569,8 @@
         a_diag, diag_cols, a_offd, offd_cols, prolong, aggregate, send_rows
     )
     gathered = gathered.reshape(2 * NZ * NY, ROWS, T)
-    offd = offd_terms(me, coarse_map[0], table, cols, left, gathered, own)
-    return place_slots(swap_slices(offd))
+    sums = offd_terms(me, table, cols, left, gathered, own)
+    return place_slots(swap_slices(coarse_map[0], sums))
 
 
 def solution(mesh):

time: 78.6 us -> 75.3 us (0.958)
  Pallas kernels: 77.2 us -> 75.1 us
  local copies, waits for them, and re-layouts: 1.17 us -> 0.01 us
    pallas_call x1, Pallas kernels: 3.28 us -> 1.86 us  [place_slots(): pl.pallas_call(place_kernel, in_specs=[pl.BlockSpec(memory_space=pltpu.VM...]
    unnamed x4 -> x2, local copies, waits for them, and re-layouts: 1.17 us -> 0.01 us
    pallas_call x2, Pallas kernels: 28.8 us -> 27.9 us  [the longest x1 22.8 us: swap_slices(): pl.pallas_call(swap_kernel, in_specs=[pl.BlockSpec(memory_space=pltpu.SME...]
where the time goes in v6:
time: 75.3 us; the launch traced here: 75.1 us
  Pallas kernels  75.1 us (100%)
    pallas_call x1, Pallas kernels, gather_all(): pl.pallas_call(gather_kernel, in_specs=[smem, smem, vmem, vmem, hbm, hbm,...  45.3 us
    pallas_call x1, Pallas kernels, swap_slices(): pl.pallas_call(swap_kernel, in_specs=[pl.BlockSpec(memory_space=pltpu.SME...  22.8 us
    pallas_call x1, Pallas kernels, offd_terms(): pl.pallas_call(offd_kernel, in_specs=[smem, smem, smem, vmem, vmem, vmem]...  5.1 us
    pallas_call x1, Pallas kernels, place_slots(): pl.pallas_call(place_kernel, in_specs=[pl.BlockSpec(memory_space=pltpu.VM...  1.86 us

profile of v6, /device:TPU:1, one launch (start us, length us, event | category | flops | bytes accessed | tf_op | source)
XLA Modules:
  0.0 75.1 jit_solution(10858078972751177008)
XLA Ops:
  0.0 45.3 %gather_all.1 = (bf16[2,8,4,528,128]{4,3,2,1,0:T(8,128)(2,1)S(1)}, bf16[4,8,3,256,128]{4,3,2,1,0:T(8,128)(2,1)S(1)}, f32[128,128]{1,0:T(8,128)S(1)}, s32[64,128]{1,0:T(8,128)S(1)}, s32[4,8,128]{2,1,0:T(8,128)S(1)}) custom-call(s32[2,8]{1,0:T(2,128)} %bitcast.14, s32[3,8]{1,0:T(4,128)} %bitcast.11, s32[3,8]{1,0:T(4,128)} %bitcast.12, s32[4,64]{1,0:T(4,128)} %bitcast.13, ...), custom_call_target="tpu_custom_call" | custom-call | tf_op jit(solution)/shard_map/gather_all/pallas_call | solution.py:366
  45.3 0.0 copy-start
  45.3 5.1 %offd_terms.1.acc = f32[64,128,128]{2,1,0:T(8,128)S(1)} custom-call(s32[1]{0:T(128)} %bitcast.1.me_ref, s32[64,128]{1,0:T(8,128)S(1)} %get-tuple-element.10.tbl_ref, s32[4,8,128]{2,1,0:T(8,128)S(1)} %get-tuple-element.11.cols_ref, bf16[4,8,3,256,128]{4,3,2,1,0:T(8,128)(2,1)S(1)} %get-tuple-element.12.l_ref, bf16[64,528,128]{2,1,0:T(8,128)(2,1)S(1)} %bitcast.9, ...), custom_call_target="tpu_custom_call" | custom-call | tf_op jit(solution)/shard_map/offd_terms/pallas_call | solution.py:438
  50.4 0.0 copy-done
  50.4 22.8 %swap_slices.1.x_ref = bf16[4,49,32,128]{3,2,1,0:T(8,128)(2,1)S(1)} custom-call(s32[98]{0:T(128)S(1)} %bitcast.10, f32[64,128,128]{2,1,0:T(8,128)S(1)} %offd_terms.1.acc), custom_call_target="tpu_custom_call" | custom-call | tf_op jit(solution)/shard_map/swap_slices/pallas_call | solution.py:503
  73.3 1.9 %place_slots.1 = bf16[2,98,32,128]{3,2,1,0:T(8,128)(2,1)} custom-call(bf16[4,49,32,128]{3,2,1,0:T(8,128)(2,1)S(1)} %swap_slices.1.x_ref), custom_call_target="tpu_custom_call" | custom-call | tf_op jit(solution)/shard_map/place_slots/pallas_call | solution.py:553
Async XLA Ops:
  45.3 5.1 %copy-start = (s32[1,98]{1,0:T(1,128)S(1)}, s32[1,98]{1,0:T(1,128)}, u32[]{:S(2)}) copy-start(s32[1,98]{1,0:T(1,128)} %param.16) | copy-start | bytes 1180

commit v7 on v6

--- a/solution.py
+++ b/solution.py
@@ -9,7 +9,6 @@
 
 CR1 = 2
 T = 128
-H = T // 2
 
 
 ROWS = 528
@@ -84,7 +83,7 @@
 def gather_kernel(
     agg_ref, dcols_ref, ocols_ref, srows_ref, p_hbm, ad_hbm, ao_hbm,
     gath, left, own_ref, tbl_ref, cols_ref,
-    p_ref, ad_ref, mine, stage, tiles, ordered, left_t, a_all, dacc, dsend, drecv, ctab,
+    p_ref, ad_ref, mine, stage, ordered, right_t, a_all, dacc, drecv, ctab,
     ssem, rsem, xs_sem, xr_sem, lsem,
 ):
     me = lax.axis_index("rows")
@@ -151,7 +150,6 @@
     def c_copy(d):
         return remote(ctab.at[0], ctab.at[d], xs_sem.at[5 + d], xr_sem.at[5 + d], link_to[d])
 
-    lane = lax.broadcasted_iota(jnp.int32, (T, T), 1)
     rows = p_hbm.shape[0]
     stage[...] = jnp.zeros_like(stage)
     stage[0 : srows_ref.shape[0], 0 : srows_ref.shape[1]] = srows_ref[...].astype(jnp.float32)
@@ -161,18 +159,14 @@
         a_send(name)
     loads[0].wait()
 
-    def tile(i, a):
-        flip = agg_ref[0, i] == a
-        return jnp.where(flip, p_ref[i, 0], p_ref[i, 1]).astype(jnp.float32)
-
-    for p in range(rows // 2):
-        pair = None
-        for r in range(2):
-            for a in range(2):
-                at = r * 64 + a * 32
-                moved = pltpu.roll(tile(2 * p + r, a), lax.rem(at + T - 32 * x, T), 1)
-                pair = moved if pair is None else jnp.where(lane >= at, moved, pair)
-        mine[p * T : (p + 1) * T, :] = pair.astype(mine.dtype)
+    for i in range(rows):
+        for a in range(2):
+            tile = jnp.where(agg_ref[0, i] == a, p_ref[i, 0], p_ref[i, 1])
+            ordered[i, :, a * T : (a + 1) * T] = tile
+            flat = tile.T
+            for g in range(4):
+                right_t[i, g * 64 + a * 32 : g * 64 + a * 32 + 32, :] = flat[g * 32 : (g + 1) * 32]
+        mine[i * 64 : (i + 1) * 64, :] = right_t[i, pl.ds(pl.multiple_of(x * 64, 64), 64), :]
     mine[4 * T :, :] = stage[...].astype(mine.dtype)
 
     plan = flood_plan()
@@ -237,29 +231,18 @@
 
     per = ao_hbm.shape[1]
 
-    def order_rows(lo, hi):
-        def row(i, _):
-            zero, one = tile(i, 0), tile(i, 1)
-            tiles[0] = zero.astype(tiles.dtype)
-            tiles[1] = one.astype(tiles.dtype)
-            left_t[i, :T] = tiles[0].T
-            left_t[i, T:] = tiles[1].T
-            z32, z64, z96 = (pltpu.roll(zero, s, 1) for s in (32, 64, 96))
-            o32, o64, o96 = (pltpu.roll(one, s, 1) for s in (32, 64, 96))
-            low = jnp.where(lane < 32, zero, jnp.where(lane < 64, o32, jnp.where(lane < 96, z32, o64)))
-            top = jnp.where(lane < 32, z64, jnp.where(lane < 64, o96, jnp.where(lane < 96, z96, one)))
-            ordered[i, :, :T] = low.astype(ordered.dtype)
-            ordered[i, :, T:] = top.astype(ordered.dtype)
-            return 0
-
-        lax.fori_loop(lo, hi, row, 0)
+    def transposed_left(tile, i):
+        return lax.dot_general(
+            tile, ordered[i], (((0,), (0,)), ((), ())), preferred_element_type=jnp.float32
+        ).astype(jnp.bfloat16)
 
     def diag_rows(lo, hi):
         def row(i, _):
             for k in range(per):
-                part = jnp.dot(left_t[i], ad_ref[i, k], preferred_element_type=jnp.float32)
                 dacc[...] += jnp.dot(
-                    part.astype(jnp.bfloat16), ordered[dcols_ref[k, i]], preferred_element_type=jnp.float32
+                    right_t[dcols_ref[k, i]],
+                    transposed_left(ad_ref[i, k], i),
+                    preferred_element_type=jnp.float32,
                 )
             return 0
 
@@ -268,27 +251,20 @@
     def left_rows(slot, part):
         def row(i, _):
             for k in range(per):
-                left[slot, i, k] = jnp.dot(
-                    left_t[i], a_all[slot, i, k], preferred_element_type=jnp.float32
-                ).astype(left.dtype)
+                left[slot, i, k] = transposed_left(a_all[slot, i, k], i)
             return 0
 
         lax.fori_loop(part * half, part * half + half, row, 0)
+
+    def share_of(quarter):
+        return pl.ds(pl.multiple_of(quarter * 64, 64), 64)
 
     def d_copy(d):
         return remote(
-            dsend.at[xat[d]], drecv.at[d - 1], xs_sem.at[8 + d], xr_sem.at[8 + d], link_to[d]
+            dacc.at[share_of(xat[d])], drecv.at[d - 1], xs_sem.at[8 + d], xr_sem.at[8 + d], link_to[d]
         )
 
     def send_diag():
-        for q in range(4):
-            at = slice((q // 2) * T, (q // 2 + 1) * T)
-            zero, one = dacc[:T, at], dacc[T:, at]
-            if q % 2 == 0:
-                one = pltpu.roll(one, H, 1)
-            else:
-                zero = pltpu.roll(zero, H, 1)
-            dsend[q] = jnp.where(lane < H, zero, one)
         for d in (1, 2, 3):
             copy = d_copy(d)
             copy.start()
@@ -303,7 +279,6 @@
         dacc[...] = jnp.zeros_like(dacc)
         loads[1].wait()
         loads[2].wait()
-        order_rows(0, rows)
 
     events = [(t, 1, name) for name, t in flood_order(plan).items()]
     steps = [
@@ -333,7 +308,7 @@
         a_take(name)
         left_rows(2, part)
 
-    total = dsend[x]
+    total = dacc[share_of(x), :]
     for d in (1, 2, 3):
         d_copy(d).wait_recv()
         total = total + drecv[d - 1]
@@ -369,8 +344,8 @@
         out_specs=[vmem, vmem, vmem, vmem, vmem],
         out_shape=[
             jax.ShapeDtypeStruct((2, NZ, NY, ROWS, T), bf16),
-            jax.ShapeDtypeStruct((4, rows, per, 2 * T, T), bf16),
-            jax.ShapeDtypeStruct((T, T), f32),
+            jax.ShapeDtypeStruct((4, rows, per, T, 2 * T), bf16),
+            jax.ShapeDtypeStruct((64, 2 * T), f32),
             jax.ShapeDtypeStruct((2 * NZ * NY, T), jnp.int32),
             jax.ShapeDtypeStruct((4, 8, T), jnp.int32),
         ],
@@ -379,13 +354,11 @@
             pltpu.VMEM((rows, per, T, T), bf16),
             pltpu.VMEM((ROWS, T), bf16),
             pltpu.VMEM((16, T), f32),
-            pltpu.VMEM((2, T, T), bf16),
             pltpu.VMEM((rows, T, 2 * T), bf16),
             pltpu.VMEM((rows, 2 * T, T), bf16),
             pltpu.VMEM((4, rows, per, T, T), bf16),
             pltpu.VMEM((2 * T, 2 * T), f32),
-            pltpu.VMEM((4, T, T), f32),
-            pltpu.VMEM((3, T, T), f32),
+            pltpu.VMEM((3, 64, 2 * T), f32),
             pltpu.VMEM((4, 8, T), jnp.int32),
             pltpu.SemaphoreType.DMA((copies,)),
             pltpu.SemaphoreType.DMA((copies,)),
@@ -411,7 +384,6 @@
 
 def offd_kernel(me_ref, tbl_ref, cols_ref, l_ref, gath_ref, d_ref, acc):
     groups, rows, per, _, _ = l_ref.shape
-    high = lax.broadcasted_iota(jnp.int32, (T, T), 1) >= H
     acc[...] = jnp.zeros_like(acc)
 
     def row(i, _):
@@ -419,13 +391,10 @@
             g, k = t // per, t % per
             col = cols_ref[g, k, i]
             slot = slot_of(col // 4)
-            sent = tbl_ref[slot, lax.rem(col, 4)]
-            odd = lax.rem(sent, 2) == 1
-            right = gath_ref[slot, pl.ds(pl.multiple_of((sent // 2) * T, T), T), :]
-            y = jnp.dot(l_ref[g, i, k], right, preferred_element_type=jnp.float32)
-            kept = jnp.where(odd, y[T:], y[:T])
-            moved = jnp.where(odd, y[:T], y[T:])
-            acc[slot] += jnp.where(high == odd, kept, pltpu.roll(moved, H, 1))
+            at = pl.multiple_of(tbl_ref[slot, lax.rem(col, 4)] * 64, 64)
+            acc[slot] += jnp.dot(
+                gath_ref[slot, pl.ds(at, 64), :], l_ref[g, i, k], preferred_element_type=jnp.float32
+            )
         return 0
 
     lax.fori_loop(0, rows, row, 0, unroll=2)
@@ -439,7 +408,7 @@
         offd_kernel,
         in_specs=[smem, smem, smem, vmem, vmem, vmem],
         out_specs=vmem,
-        out_shape=jax.ShapeDtypeStruct((gathered.shape[0], T, T), jnp.float32),
+        out_shape=jax.ShapeDtypeStruct((gathered.shape[0], 64, 2 * T), jnp.float32),
         compiler_params=pltpu.CompilerParams(vmem_limit_bytes=32 << 20),
         name="offd_terms",
     )(me, table, cols, left, gathered, own)
@@ -456,16 +425,14 @@
     chunks = ssem.shape[1]
     step = pairs // chunks
 
-    lane = lax.broadcasted_iota(jnp.int32, (T, T), 1)
-    even = lax.rem(lane // 32, 2) == 0
-
     def pack(p):
-        def part(j):
-            gid = map_ref[2 * p + j]
-            value = acc[slot_of(gid // CR1)]
-            return jnp.where(lax.rem(gid, CR1) == j, value, pltpu.roll(value, 32 if j else T - 32, 1))
-
-        both = jnp.where(even, part(0), part(1)).astype(src.dtype)
+        items = []
+        for a in range(CR1):
+            for j in range(2):
+                gid = map_ref[2 * p + j]
+                both = acc[slot_of(gid // CR1), :, a * T : (a + 1) * T]
+                items.append(jnp.where(lax.rem(gid, CR1) == 0, both[:32], both[32:]))
+        both = jnp.concatenate(items, axis=0).T.astype(src.dtype)
         for g in range(src.shape[0]):
             src[g, p] = both[g * quarter : (g + 1) * quarter]
 

time: 75.3 us -> 72.8 us (0.967)
  Pallas kernels: 75.1 us -> 72.6 us
    pallas_call x1, Pallas kernels: 5.1 us -> 3.55 us  [offd_terms(): pl.pallas_call(offd_kernel, in_specs=[smem, smem, smem, vmem, vmem, vmem]...]
    pallas_call x1, Pallas kernels: 22.8 us -> 21.8 us  [swap_slices(): pl.pallas_call(swap_kernel, in_specs=[pl.BlockSpec(memory_space=pltpu.SME...]
where the time goes in v7:
time: 72.8 us; the launch traced here: 72.7 us
  Pallas kernels  72.6 us (100%)
    pallas_call x1, Pallas kernels, gather_all(): pl.pallas_call(gather_kernel, in_specs=[smem, smem, vmem, vmem, hbm, hbm,...  45.4 us
    pallas_call x1, Pallas kernels, swap_slices(): pl.pallas_call(swap_kernel, in_specs=[pl.BlockSpec(memory_space=pltpu.SME...  21.8 us
    pallas_call x1, Pallas kernels, offd_terms(): pl.pallas_call(offd_kernel, in_specs=[smem, smem, smem, vmem, vmem, vmem]...  3.55 us
    pallas_call x1, Pallas kernels, place_slots(): pl.pallas_call(place_kernel, in_specs=[pl.BlockSpec(memory_space=pltpu.VM...  1.86 us

profile of v7, /device:TPU:1, one launch (start us, length us, event | category | flops | bytes accessed | tf_op | source)
XLA Modules:
  0.0 72.7 jit_solution(1945942509515728804)
XLA Ops:
  0.0 45.4 %gather_all.1 = (bf16[2,8,4,528,128]{4,3,2,1,0:T(8,128)(2,1)S(1)}, bf16[4,8,3,128,256]{4,3,2,1,0:T(8,128)(2,1)S(1)}, f32[64,256]{1,0:T(8,128)S(1)}, s32[64,128]{1,0:T(8,128)S(1)}, s32[4,8,128]{2,1,0:T(8,128)S(1)}) custom-call(s32[2,8]{1,0:T(2,128)} %bitcast.14, s32[3,8]{1,0:T(4,128)} %bitcast.11, s32[3,8]{1,0:T(4,128)} %bitcast.12, s32[4,64]{1,0:T(4,128)} %bitcast.13, ...), custom_call_target="tpu_custom_call" | custom-call | tf_op jit(solution)/shard_map/gather_all/pallas_call | solution.py:341
  45.4 0.0 copy-start
  45.4 3.6 %offd_terms.1.acc = f32[64,64,256]{2,1,0:T(8,128)S(1)} custom-call(s32[1]{0:T(128)} %bitcast.1.me_ref, s32[64,128]{1,0:T(8,128)S(1)} %get-tuple-element.10.tbl_ref, s32[4,8,128]{2,1,0:T(8,128)S(1)} %get-tuple-element.11.cols_ref, bf16[4,8,3,128,256]{4,3,2,1,0:T(8,128)(2,1)S(1)} %get-tuple-element.12.l_ref, bf16[64,528,128]{2,1,0:T(8,128)(2,1)S(1)} %bitcast.9, ...), custom_call_target="tpu_custom_call" | custom-call | tf_op jit(solution)/shard_map/offd_terms/pallas_call | solution.py:407
  49.0 0.0 copy-done
  49.0 21.8 %swap_slices.1.x_ref = bf16[4,49,32,128]{3,2,1,0:T(8,128)(2,1)S(1)} custom-call(s32[98]{0:T(128)S(1)} %bitcast.10, f32[64,64,256]{2,1,0:T(8,128)S(1)} %offd_terms.1.acc), custom_call_target="tpu_custom_call" | custom-call | tf_op jit(solution)/shard_map/swap_slices/pallas_call | solution.py:470
  70.8 1.9 %place_slots.1 = bf16[2,98,32,128]{3,2,1,0:T(8,128)(2,1)} custom-call(bf16[4,49,32,128]{3,2,1,0:T(8,128)(2,1)S(1)} %swap_slices.1.x_ref), custom_call_target="tpu_custom_call" | custom-call | tf_op jit(solution)/shard_map/place_slots/pallas_call | solution.py:520
Async XLA Ops:
  45.4 3.6 %copy-start = (s32[1,98]{1,0:T(1,128)S(1)}, s32[1,98]{1,0:T(1,128)}, u32[]{:S(2)}) copy-start(s32[1,98]{1,0:T(1,128)} %param.16) | copy-start | bytes 1180

commit v8 on v7

--- a/solution.py
+++ b/solution.py
@@ -12,13 +12,19 @@
 
 
 ROWS = 528
-ZR = 320
+ZR = 288
 NZ, NY = 8, 4
 MESH = pl.DeviceIdType.MESH
 PARTS = {"z": (0, ZR), "za": (0, ZR // 2), "zb": (ZR // 2, ZR // 2),
          "y": (ZR, ROWS - ZR), "ya": (ZR, 112), "yb": (ZR + 112, ROWS - ZR - 112)}
 DZ = (0, 1, -1, 2, -2, 3, -3, 4)
 LATE_UP = (0, 1, 2, 3)
+SHARES = [
+    (kind, dz, dy)
+    for dz in DZ
+    for kind in ("z", "y")
+    for dy in ((None,) if abs(dz) < 3 else (0, 1, -1, 2))
+]
 
 
 def flood_plan():
@@ -59,23 +65,38 @@
     return plan
 
 
-def flood_order(plan):
+def flood_rank(plan):
+    kids = {}
+    for name, item in plan.items():
+        for a in item[4]:
+            kids.setdefault(a, []).append(name)
+    memo = {}
+
+    def depth(name):
+        if name not in memo:
+            memo[name] = 1 + max([depth(k) for k in kids.get(name, [])], default=0)
+        return memo[name]
+
+    kind = {"Y": 0, "Z": 1, "YZ": 2, "ZY": 3}
+    return {n: (-depth(n), kind[n[0]], abs(n[1]), str(n)) for n in plan}
+
+
+def flood_order(plan, latency=2.5, rate=49e3):
+    rank = flood_rank(plan)
     free = {}
     arrive, waiting = {}, dict(plan)
-    rank = {"Y": 0, "Z": 1, "YZ": 2, "ZY": 3}
-    while len(arrive) < len(plan):
+    while waiting:
         best = None
         for name, (link, _, _, part, after) in waiting.items():
             if any(a not in arrive for a in after):
                 continue
             start = max([arrive[a] for a in after] + [free.get(link, 0.0)])
-            key = (start, rank[name[0]], abs(name[1]), str(name))
+            key = (start,) + rank[name]
             if best is None or key < best[0]:
-                best = (key, name, start, link, part)
-        _, name, start, link, part = best
-        end = start + PARTS[part][1] * 256 / 50e3
-        free[link] = end
-        arrive[name] = end + 1.5
+                best = (key, name, start, link, PARTS[part][1] * 256 / rate)
+        _, name, start, link, took = best
+        free[link] = start + took
+        arrive[name] = start + took + latency
         del waiting[name]
     return arrive
 
@@ -187,35 +208,40 @@
 
     started = set()
 
+    rank = flood_rank(plan)
+
     def start_ready(have):
-        order = {"Y": 0, "Z": 1, "YZ": 2, "ZY": 3}
-        for name in sorted(plan, key=lambda n: (order[n[0]], abs(n[1]), str(n))):
+        for name in sorted(plan, key=rank.get):
             if name not in started and all(a in have for a in plan[name][4]):
                 started.add(name)
                 copy = f_copy(name, True)
                 copy.start()
                 sends.append(copy)
 
-    def s_copy(kind, dz, sending):
-        i = len(names) + DZ.index(dz) * 2 + (kind == "y")
-        plane = core if sending else 1 - core
-        ref = gath.at[plane, lax.rem(z + (NZ - dz), NZ), :, pl.ds(*PARTS[kind])]
+    def s_copy(key, sending):
+        kind, dz, dy = key
+        i = len(names) + SHARES.index(key)
+        at = pl.ds(*PARTS[kind])
+        plane = gath.at[core if sending else 1 - core, lax.rem(z + (NZ - dz), NZ)]
+        ref = plane.at[:, at] if dy is None else plane.at[lax.rem(y + (NY - dy), NY), at]
         return remote(ref, ref, ssem.at[i], rsem.at[i], link_to["core"])
 
     need = {}
-    for dz in DZ:
+    for kind, dz, dy in SHARES:
         zs = [] if dz == 0 else ([("Z", dz)] if dz != 4 else [("Z", 4, 1), ("Z", 4, -1)])
-        need[("z", dz)] = zs + [("ZY", dz, s) for s in (1, -1, 2)]
-        need[("y", dz)] = (
-            [("Y", 1), ("Y", -1), ("Y", 2, 1), ("Y", 2, -1)]
-            if dz == 0
-            else [("YZ", dz, s) for s in (0, 1, -1, 2)]
-        )
+        parts = {}
+        if kind == "z":
+            parts = {0: zs, **{d: [("ZY", dz, d)] for d in (1, -1, 2)}}
+        elif dz == 0:
+            parts = {0: [], 1: [("Y", 1)], -1: [("Y", -1)], 2: [("Y", 2, 1), ("Y", 2, -1)]}
+        else:
+            parts = {d: [("YZ", dz, d)] for d in (0, 1, -1, 2)}
+        need[kind, dz, dy] = sum(parts.values(), []) if dy is None else parts[dy]
 
     def share(have):
         for key in list(need):
             if all(a in have for a in need[key]):
-                copy = s_copy(*key, True)
+                copy = s_copy(key, True)
                 copy.start()
                 sends.append(copy)
                 del need[key]
@@ -282,8 +308,15 @@
 
     events = [(t, 1, name) for name, t in flood_order(plan).items()]
     steps = [
-        (0.0, begin), (1.5, lambda: diag_rows(0, 2)), (3.5, lambda: diag_rows(2, 4)),
-        (5.5, lambda: diag_rows(4, 6)), (7.5, lambda: diag_rows(6, 8)),
+        (0.0, begin),
+        (0.5, lambda: diag_rows(0, 1)),
+        (1.4, lambda: diag_rows(1, 2)),
+        (2.3, lambda: diag_rows(2, 3)),
+        (3.2, lambda: diag_rows(3, 4)),
+        (4.1, lambda: diag_rows(4, 5)),
+        (5.0, lambda: diag_rows(5, 6)),
+        (5.9, lambda: diag_rows(6, 7)),
+        (6.8, lambda: diag_rows(7, 8)),
         (7.6, send_diag),
         (9.5, lambda: a_take(("r", 0), ("r", 2))), (9.6, lambda: a_take(("l", 1), ("l", 2))),
         (10.5, lambda: left_rows(0, 0)), (12.0, lambda: left_rows(0, 1)),
@@ -316,9 +349,8 @@
     own_ref[...] = total
     cols_ref[...] = ctab[...]
 
-    for dz in DZ:
-        for kind in ("z", "y"):
-            s_copy(kind, dz, False).wait_recv()
+    for key in SHARES:
+        s_copy(key, False).wait_recv()
     tail = gath[:, :, :, 4 * T :, :].reshape(2 * NZ * NY * 16, T)
     pick = (lax.broadcasted_iota(jnp.int32, (T, T), 0) == me).astype(jnp.bfloat16)
     spread = jnp.dot(tail, pick, preferred_element_type=jnp.float32).reshape(2 * NZ * NY, 16, T)
@@ -336,7 +368,7 @@
     vmem = pl.BlockSpec(memory_space=pltpu.VMEM)
     smem = pl.BlockSpec(memory_space=pltpu.SMEM)
     hbm = pl.BlockSpec(memory_space=pltpu.HBM)
-    copies = len(flood_plan()) + 2 * len(DZ)
+    copies = len(flood_plan()) + len(SHARES)
     bf16, f32 = jnp.bfloat16, jnp.float32
     return pl.pallas_call(
         gather_kernel,

time: 72.8 us -> 69.4 us (0.953); the launches traced: 72.7 us -> 68.5 us
  Pallas kernels: 72.6 us -> 68.4 us
    pallas_call x1, Pallas kernels: 45.4 us -> 42.7 us  [gather_all(): pl.pallas_call(gather_kernel, in_specs=[smem, smem, vmem, vmem, hbm, hbm,...]
    pallas_call x1, Pallas kernels: 21.8 us -> 20.3 us  [swap_slices(): pl.pallas_call(swap_kernel, in_specs=[pl.BlockSpec(memory_space=pltpu.SME...]
where the time goes in v8:
time: 69.4 us; the launch traced here: 68.5 us
  Pallas kernels  68.4 us (99%)
    pallas_call x1, Pallas kernels, gather_all(): pl.pallas_call(gather_kernel, in_specs=[smem, smem, vmem, vmem, hbm, hbm,...  42.7 us
    pallas_call x1, Pallas kernels, swap_slices(): pl.pallas_call(swap_kernel, in_specs=[pl.BlockSpec(memory_space=pltpu.SME...  20.3 us
    pallas_call x1, Pallas kernels, offd_terms(): pl.pallas_call(offd_kernel, in_specs=[smem, smem, smem, vmem, vmem, vmem]...  3.56 us
    pallas_call x1, Pallas kernels, place_slots(): pl.pallas_call(place_kernel, in_specs=[pl.BlockSpec(memory_space=pltpu.VM...  1.86 us

profile of v8, /device:TPU:1, one launch (start us, length us, event | category | flops | bytes accessed | tf_op | source)
XLA Modules:
  0.0 68.5 jit_solution(13726961414845997381)
XLA Ops:
  0.0 42.7 %gather_all.1 = (bf16[2,8,4,528,128]{4,3,2,1,0:T(8,128)(2,1)S(1)}, bf16[4,8,3,128,256]{4,3,2,1,0:T(8,128)(2,1)S(1)}, f32[64,256]{1,0:T(8,128)S(1)}, s32[64,128]{1,0:T(8,128)S(1)}, s32[4,8,128]{2,1,0:T(8,128)S(1)}) custom-call(s32[2,8]{1,0:T(2,128)} %bitcast.14, s32[3,8]{1,0:T(4,128)} %bitcast.11, s32[3,8]{1,0:T(4,128)} %bitcast.12, s32[4,64]{1,0:T(4,128)} %bitcast.13, ...), custom_call_target="tpu_custom_call" | custom-call | tf_op jit(solution)/shard_map/gather_all/pallas_call | solution.py:373
  42.7 0.0 copy-start
  42.7 3.6 %offd_terms.1.acc = f32[64,64,256]{2,1,0:T(8,128)S(1)} custom-call(s32[1]{0:T(128)} %bitcast.1.me_ref, s32[64,128]{1,0:T(8,128)S(1)} %get-tuple-element.10.tbl_ref, s32[4,8,128]{2,1,0:T(8,128)S(1)} %get-tuple-element.11.cols_ref, bf16[4,8,3,128,256]{4,3,2,1,0:T(8,128)(2,1)S(1)} %get-tuple-element.12.l_ref, bf16[64,528,128]{2,1,0:T(8,128)(2,1)S(1)} %bitcast.9, ...), custom_call_target="tpu_custom_call" | custom-call | tf_op jit(solution)/shard_map/offd_terms/pallas_call | solution.py:439
  46.3 0.0 copy-done
  46.3 20.3 %swap_slices.1.x_ref = bf16[4,49,32,128]{3,2,1,0:T(8,128)(2,1)S(1)} custom-call(s32[98]{0:T(128)S(1)} %bitcast.10, f32[64,64,256]{2,1,0:T(8,128)S(1)} %offd_terms.1.acc), custom_call_target="tpu_custom_call" | custom-call | tf_op jit(solution)/shard_map/swap_slices/pallas_call | solution.py:502
  66.6 1.9 %place_slots.1 = bf16[2,98,32,128]{3,2,1,0:T(8,128)(2,1)} custom-call(bf16[4,49,32,128]{3,2,1,0:T(8,128)(2,1)S(1)} %swap_slices.1.x_ref), custom_call_target="tpu_custom_call" | custom-call | tf_op jit(solution)/shard_map/place_slots/pallas_call | solution.py:552
Async XLA Ops:
  42.7 3.6 %copy-start = (s32[1,98]{1,0:T(1,128)S(1)}, s32[1,98]{1,0:T(1,128)}, u32[]{:S(2)}) copy-start(s32[1,98]{1,0:T(1,128)} %param.16) | copy-start | bytes 1180

commit v9 on v8

--- a/solution.py
+++ b/solution.py
@@ -318,7 +318,7 @@
         (5.9, lambda: diag_rows(6, 7)),
         (6.8, lambda: diag_rows(7, 8)),
         (7.6, send_diag),
-        (9.5, lambda: a_take(("r", 0), ("r", 2))), (9.6, lambda: a_take(("l", 1), ("l", 2))),
+        (11.5, lambda: a_take(("r", 0), ("r", 2))), (11.6, lambda: a_take(("l", 1), ("l", 2))),
         (10.5, lambda: left_rows(0, 0)), (12.0, lambda: left_rows(0, 1)),
         (13.5, lambda: left_rows(1, 0)), (15.0, lambda: left_rows(3, 1)),
         (18.0, lambda: (a_take(("r", 1)), left_rows(1, 1))),
@@ -429,7 +429,7 @@
             )
         return 0
 
-    lax.fori_loop(0, rows, row, 0, unroll=2)
+    lax.fori_loop(0, rows, row, 0, unroll=4)
     acc[slot_of(me_ref[0])] = d_ref[...]
 
 
@@ -454,8 +454,8 @@
     for d in (2, 1, 3):
         pl.semaphore_signal(barrier, inc=1, device_id=(me, at[d]), device_id_type=MESH)
     pairs, quarter = src.shape[1], src.shape[2]
-    chunks = ssem.shape[1]
-    step = pairs // chunks
+    cuts = [0, 2, 7, 21, 35, pairs]
+    chunks = len(cuts) - 1
 
     def pack(p):
         items = []
@@ -469,7 +469,7 @@
             src[g, p] = both[g * quarter : (g + 1) * quarter]
 
     def remote(d, c, a, b):
-        piece = pl.ds(c * step, step)
+        piece = pl.ds(cuts[c], cuts[c + 1] - cuts[c])
         return pltpu.make_async_remote_copy(
             src_ref=a.at[piece], dst_ref=b.at[piece],
             send_sem=ssem.at[d - 1, c], recv_sem=rsem.at[d - 1, c],
@@ -477,7 +477,7 @@
         )
 
     for c in range(chunks):
-        for p in range(c * step, (c + 1) * step):
+        for p in range(cuts[c], cuts[c + 1]):
             pack(p)
         if c == 0:
             pl.semaphore_wait(barrier, 3)
@@ -498,7 +498,7 @@
 def swap_slices(col_map, sums):
     vmem = pl.BlockSpec(memory_space=pltpu.VMEM)
     shape = (4, col_map.shape[0] // 2, T // 4, T)
-    chunks = 7
+    chunks = 5
     return pl.pallas_call(
         swap_kernel,
         in_specs=[pl.BlockSpec(memory_space=pltpu.SMEM), vmem],

time: 69.4 us -> 69 us (level)
  no operation moved by 1% of the time
where the time goes in v9:
time: 69 us; the launch traced here: 68.1 us
  Pallas kernels  68 us (99%)
    pallas_call x1, Pallas kernels, gather_all(): pl.pallas_call(gather_kernel, in_specs=[smem, smem, vmem, vmem, hbm, hbm,...  42.7 us
    pallas_call x1, Pallas kernels, swap_slices(): pl.pallas_call(swap_kernel, in_specs=[pl.BlockSpec(memory_space=pltpu.SME...  20.2 us
    pallas_call x1, Pallas kernels, offd_terms(): pl.pallas_call(offd_kernel, in_specs=[smem, smem, smem, vmem, vmem, vmem]...  3.28 us
    pallas_call x1, Pallas kernels, place_slots(): pl.pallas_call(place_kernel, in_specs=[pl.BlockSpec(memory_space=pltpu.VM...  1.86 us

profile of v9, /device:TPU:1, one launch (start us, length us, event | category | flops | bytes accessed | tf_op | source)
XLA Modules:
  0.0 68.1 jit_solution(12743751085211926087)
XLA Ops:
  0.0 42.7 %gather_all.1 = (bf16[2,8,4,528,128]{4,3,2,1,0:T(8,128)(2,1)S(1)}, bf16[4,8,3,128,256]{4,3,2,1,0:T(8,128)(2,1)S(1)}, f32[64,256]{1,0:T(8,128)S(1)}, s32[64,128]{1,0:T(8,128)S(1)}, s32[4,8,128]{2,1,0:T(8,128)S(1)}) custom-call(s32[2,8]{1,0:T(2,128)} %bitcast.14, s32[3,8]{1,0:T(4,128)} %bitcast.11, s32[3,8]{1,0:T(4,128)} %bitcast.12, s32[4,64]{1,0:T(4,128)} %bitcast.13, ...), custom_call_target="tpu_custom_call" | custom-call | tf_op jit(solution)/shard_map/gather_all/pallas_call | solution.py:373
  42.7 0.0 copy-start
  42.7 3.3 %offd_terms.1.acc = f32[64,64,256]{2,1,0:T(8,128)S(1)} custom-call(s32[1]{0:T(128)} %bitcast.1.me_ref, s32[64,128]{1,0:T(8,128)S(1)} %get-tuple-element.10.tbl_ref, s32[4,8,128]{2,1,0:T(8,128)S(1)} %get-tuple-element.11.cols_ref, bf16[4,8,3,128,256]{4,3,2,1,0:T(8,128)(2,1)S(1)} %get-tuple-element.12.l_ref, bf16[64,528,128]{2,1,0:T(8,128)(2,1)S(1)} %bitcast.9, ...), custom_call_target="tpu_custom_call" | custom-call | tf_op jit(solution)/shard_map/offd_terms/pallas_call | solution.py:439
  46.0 0.0 copy-done
  46.0 20.2 %swap_slices.1.x_ref = bf16[4,49,32,128]{3,2,1,0:T(8,128)(2,1)S(1)} custom-call(s32[98]{0:T(128)S(1)} %bitcast.10, f32[64,64,256]{2,1,0:T(8,128)S(1)} %offd_terms.1.acc), custom_call_target="tpu_custom_call" | custom-call | tf_op jit(solution)/shard_map/swap_slices/pallas_call | solution.py:502
  66.2 1.9 %place_slots.1 = bf16[2,98,32,128]{3,2,1,0:T(8,128)(2,1)} custom-call(bf16[4,49,32,128]{3,2,1,0:T(8,128)(2,1)S(1)} %swap_slices.1.x_ref), custom_call_target="tpu_custom_call" | custom-call | tf_op jit(solution)/shard_map/place_slots/pallas_call | solution.py:552
Async XLA Ops:
  42.7 3.3 %copy-start = (s32[1,98]{1,0:T(1,128)S(1)}, s32[1,98]{1,0:T(1,128)}, u32[]{:S(2)}) copy-start(s32[1,98]{1,0:T(1,128)} %param.16) | copy-start | bytes 1180

commit v10 on v9

--- a/solution.py
+++ b/solution.py
@@ -429,7 +429,7 @@
             )
         return 0
 
-    lax.fori_loop(0, rows, row, 0, unroll=4)
+    lax.fori_loop(0, rows, row, 0, unroll=8)
     acc[slot_of(me_ref[0])] = d_ref[...]
 
 

time: 69 us -> 68.8 us (level)
  no operation moved by 1% of the time
where the time goes in v10:
time: 68.8 us; the launch traced here: 67.8 us
  Pallas kernels  67.8 us (99%)
    pallas_call x1, Pallas kernels, gather_all(): pl.pallas_call(gather_kernel, in_specs=[smem, smem, vmem, vmem, hbm, hbm,...  42.7 us
    pallas_call x1, Pallas kernels, swap_slices(): pl.pallas_call(swap_kernel, in_specs=[pl.BlockSpec(memory_space=pltpu.SME...  20.2 us
    pallas_call x1, Pallas kernels, offd_terms(): pl.pallas_call(offd_kernel, in_specs=[smem, smem, smem, vmem, vmem, vmem]...  3.05 us
    pallas_call x1, Pallas kernels, place_slots(): pl.pallas_call(place_kernel, in_specs=[pl.BlockSpec(memory_space=pltpu.VM...  1.86 us

profile of v10, /device:TPU:1, one launch (start us, length us, event | category | flops | bytes accessed | tf_op | source)
XLA Modules:
  0.0 67.8 jit_solution(12453519083301543131)
XLA Ops:
  0.0 42.7 %gather_all.1 = (bf16[2,8,4,528,128]{4,3,2,1,0:T(8,128)(2,1)S(1)}, bf16[4,8,3,128,256]{4,3,2,1,0:T(8,128)(2,1)S(1)}, f32[64,256]{1,0:T(8,128)S(1)}, s32[64,128]{1,0:T(8,128)S(1)}, s32[4,8,128]{2,1,0:T(8,128)S(1)}) custom-call(s32[2,8]{1,0:T(2,128)} %bitcast.14, s32[3,8]{1,0:T(4,128)} %bitcast.11, s32[3,8]{1,0:T(4,128)} %bitcast.12, s32[4,64]{1,0:T(4,128)} %bitcast.13, ...), custom_call_target="tpu_custom_call" | custom-call | tf_op jit(solution)/shard_map/gather_all/pallas_call | solution.py:373
  42.7 0.0 copy-start
  42.7 3.0 %offd_terms.1.acc = f32[64,64,256]{2,1,0:T(8,128)S(1)} custom-call(s32[1]{0:T(128)} %bitcast.1.me_ref, s32[64,128]{1,0:T(8,128)S(1)} %get-tuple-element.10.tbl_ref, s32[4,8,128]{2,1,0:T(8,128)S(1)} %get-tuple-element.11.cols_ref, bf16[4,8,3,128,256]{4,3,2,1,0:T(8,128)(2,1)S(1)} %get-tuple-element.12.l_ref, bf16[64,528,128]{2,1,0:T(8,128)(2,1)S(1)} %bitcast.9, ...), custom_call_target="tpu_custom_call" | custom-call | tf_op jit(solution)/shard_map/offd_terms/pallas_call | solution.py:439
  45.8 0.0 copy-done
  45.8 20.2 %swap_slices.1.x_ref = bf16[4,49,32,128]{3,2,1,0:T(8,128)(2,1)S(1)} custom-call(s32[98]{0:T(128)S(1)} %bitcast.10, f32[64,64,256]{2,1,0:T(8,128)S(1)} %offd_terms.1.acc), custom_call_target="tpu_custom_call" | custom-call | tf_op jit(solution)/shard_map/swap_slices/pallas_call | solution.py:502
  66.0 1.9 %place_slots.1 = bf16[2,98,32,128]{3,2,1,0:T(8,128)(2,1)} custom-call(bf16[4,49,32,128]{3,2,1,0:T(8,128)(2,1)S(1)} %swap_slices.1.x_ref), custom_call_target="tpu_custom_call" | custom-call | tf_op jit(solution)/shard_map/place_slots/pallas_call | solution.py:552
Async XLA Ops:
  42.7 3.1 %copy-start = (s32[1,98]{1,0:T(1,128)S(1)}, s32[1,98]{1,0:T(1,128)}, u32[]{:S(2)}) copy-start(s32[1,98]{1,0:T(1,128)} %param.16) | copy-start | bytes 1180
